TPU v7x, 512 devices: a whole 4x4x16 slice. The times are simulated.
512 devices in a mesh: band: 8 (over x_lo, y), lon: 64 (over x_hi, z, core).
Axes of the slice: x: 4 (x_hi: 2, x_lo: 2; x = x_hi * 2 + x_lo), y: 4, z: 16, core: 2. Of those that a mesh axis runs over, the one named last changes fastest.
Arguments:
- tracers: float32 [384, 1024, 128], P('band', 'lon'), may hold values from -6 to 6
- lon_offset: int32 [384, 4], P('band'), may hold values from -512 to 511
- lon_weights: float32 [4, 384, 4], P(None, 'band'), may hold values from -0.1 to 1, as said below
- lat_offset: int32 [384, 4], P('band'), may hold values from -6 to 6
- lat_weights: float32 [4, 384, 4], P(None, 'band'), may hold values from -0.1 to 1, as said below
Outputs:
- advected: float32 [384, 1024, 128], P('band', 'lon')
Inputs may be any that keep to these rules, and one draw needn't show every extreme that they name: `lon_weights`: each set of four weights sums to one. `lat_weights`: each set of four weights sums to one.
All inputs are finite; a program needn't handle non-finite values.
Results may differ from a plain program's by a relative error of at most 0.0003.
Values sent between devices are 32-bit elements; how exact they have to be, the bound alone decides.
No kernel may reach another device: no remote copies, remote signals or barrier semaphores. Data moves between devices by JAX's collectives and lax.ppermute only.
A program may use at most 64 MiB of HBM per device.

v0:
```python
import jax
import jax.numpy as jnp
from jax import lax
from jax.sharding import PartitionSpec as P

TMAX = 6


def passed_along(value, axis, steps):
    count = lax.axis_size(axis)
    pairs = [(source, (source + steps) % count) for source in range(count)]
    return lax.ppermute(value, axis, pairs)


def extended_2(cells, sides, width, closed):
    for axis, dim in sides:
        count = lax.axis_size(axis)
        ends = count if closed else count - 1
        head = lax.slice_in_dim(cells, 0, width, axis=dim)
        tail = lax.slice_in_dim(cells, cells.shape[dim] - width, cells.shape[dim], axis=dim)
        cells = jnp.concatenate(
            [
                lax.ppermute(tail, axis, [(i, (i + 1) % count) for i in range(ends)]),
                cells,
                lax.ppermute(head, axis, [((i + 1) % count, i) for i in range(ends)]),
            ],
            axis=dim,
        )
    return cells


def spread_levels(values, per_level):
    return jnp.repeat(values, per_level, axis=-1)


def zonal_pass(field, offsets, weights):
    rows, width, columns = field.shape
    levels = offsets.shape[1]
    per_level = columns // levels
    sectors = lax.axis_size("lon")
    circle = width * sectors
    wrapped = jnp.mod(offsets, circle)
    steps = spread_levels(wrapped // width, per_level)
    rest = spread_levels(wrapped % width, per_level)
    coeffs = spread_levels(weights, per_level)
    moved = field
    for bit in range(sectors.bit_length() - 1):
        other = passed_along(moved, "lon", 1 << bit)
        taken = steps // (1 << bit) % 2 == 1
        moved = jnp.where(taken[:, None, :], other, moved)
    extended = extended_2(moved, (("lon", 1),), width, True)
    target = jnp.arange(width, dtype=jnp.int32)[None, :, None, None]
    source = jnp.arange(3 * width, dtype=jnp.int32)[None, None, :, None]
    base = (width - 1 - rest)[:, None, None, :]
    banded = jnp.zeros((rows, width, 3 * width, columns), jnp.float32)
    for k in range(4):
        banded = banded + coeffs[k][:, None, None, :] * (source == target + base + k).astype(
            jnp.float32
        )
    return jnp.sum(banded * extended[:, None, :, :], axis=2)


def meridional_pass(field, offsets, weights, form, per_level):
    rows = field.shape[0]
    reach = TMAX + 2
    extended = extended_2(field, (("band", 0),), reach, False)
    total_rows = rows * lax.axis_size("band")
    first_row = lax.axis_index("band") * rows
    glob = first_row + jnp.arange(rows, dtype=jnp.int32)[:, None]
    places = jnp.arange(rows + 2 * reach, dtype=jnp.int32)[None, :, None]
    selector = jnp.zeros((rows, rows + 2 * reach, offsets.shape[1]), jnp.float32)
    for k in range(4):
        source = jnp.clip(glob - offsets + (k - 1), 0, total_rows - 1) - first_row + reach
        selector = selector + weights[k][:, None, :] * (places == source[:, None, :]).astype(
            jnp.float32
        )
    selector = spread_levels(selector, per_level)
    return jnp.einsum(form, selector, extended, precision=lax.Precision.HIGHEST)


def per_device(tracers, lon_offset, lon_weights, lat_offset, lat_weights):
    rows, width, columns = tracers.shape
    levels = lon_offset.shape[1]
    first = zonal_pass(tracers, lon_offset, lon_weights)
    second = meridional_pass(first, lat_offset, lat_weights, "jpc,pic->jic", columns // levels)
    return zonal_pass(second, lon_offset, lon_weights)


def solution(mesh):
    return jax.shard_map(
        per_device,
        mesh=mesh,
        in_specs=(
            P("band", "lon", None),
            P("band", None),
            P(None, "band", None),
            P("band", None),
            P(None, "band", None),
        ),
        out_specs=P("band", "lon", None),
        check_vma=False,
    )
```

profile of v0, /device:TPU:8, one launch (start us, length us, event | category | flops | bytes accessed | tf_op | source)
XLA Modules:
  0.0 377.2 jit_solution(6018770357073155751)
XLA Ops:
  0.0 1.9 collective-permute-start
  1.9 1.5 copy.69
  3.5 0.7 fusion.53
  4.3 14.6 %collective-permute-done = f32[48,16,128]{2,1,0:T(8,128)S(1)} collective-permute-done((f32[48,16,128]{2,1,0:T(8,128)}, f32[48,16,128]{2,1,0:T(8,128)S(1)}, u32[]{:S(2)}, u32[]{:S(2)}) %collective-permute-start) | collective-permute-done | bytes 393248 | tf_op jit(solution)/shard_map/ppermute | solution.py:12
  20.2 1.9 collective-permute-start.1
  22.1 11.4 %collective-permute-done.1 = f32[48,16,128]{2,1,0:T(8,128)S(1)} collective-permute-done((f32[48,16,128]{2,1,0:T(8,128)S(1)}, f32[48,16,128]{2,1,0:T(8,128)S(1)}, u32[]{:S(2)}, u32[]{:S(2)}) %collective-permute-start.1) | collective-permute-done | bytes 393248 | tf_op jit(solution)/shard_map/ppermute | solution.py:12
  34.8 1.9 collective-permute-start.2
  36.7 17.6 %collective-permute-done.2 = f32[48,16,128]{2,1,0:T(8,128)S(1)} collective-permute-done((f32[48,16,128]{2,1,0:T(8,128)S(1)}, f32[48,16,128]{2,1,0:T(8,128)S(1)}, u32[]{:S(2)}, u32[]{:S(2)}) %collective-permute-start.2) | collective-permute-done | bytes 393248 | tf_op jit(solution)/shard_map/ppermute | solution.py:12
  55.6 1.9 collective-permute-start.3
  57.5 36.6 %collective-permute-done.3 = f32[48,16,128]{2,1,0:T(8,128)S(1)} collective-permute-done((f32[48,16,128]{2,1,0:T(8,128)S(1)}, f32[48,16,128]{2,1,0:T(8,128)S(1)}, u32[]{:S(2)}, u32[]{:S(2)}) %collective-permute-start.3) | collective-permute-done | bytes 393248 | tf_op jit(solution)/shard_map/ppermute | solution.py:12
  95.4 1.9 collective-permute-start.4
  97.3 42.3 %collective-permute-done.4 = f32[48,16,128]{2,1,0:T(8,128)S(1)} collective-permute-done((f32[48,16,128]{2,1,0:T(8,128)S(1)}, f32[48,16,128]{2,1,0:T(8,128)S(1)}, u32[]{:S(2)}, u32[]{:S(2)}) %collective-permute-start.4) | collective-permute-done | bytes 393248 | tf_op jit(solution)/shard_map/ppermute | solution.py:12
  140.9 3.1 collective-permute-start.5
  148.0 4.0 %collective-permute-done.5 = f32[48,16,128]{2,1,0:T(8,128)S(1)} collective-permute-done((f32[48,16,128]{2,1,0:T(8,128)S(1)}, f32[48,16,128]{2,1,0:T(8,128)S(1)}, u32[]{:S(2)}, u32[]{:S(2)}) %collective-permute-start.5) | collective-permute-done | bytes 393248 | tf_op jit(solution)/shard_map/ppermute | solution.py:12
  153.4 1.9 collective-permute-start.7
  155.3 2.6 collective-permute-start.6
  157.9 0.8 iota_add_fusion
  158.9 1.7 collective-permute-done.7
  160.6 7.4 %collective-permute-done.6 = f32[48,16,128]{2,1,0:T(8,128)S(1)} collective-permute-done((f32[48,16,128]{2,1,0:T(8,128)S(1)}, f32[48,16,128]{2,1,0:T(8,128)S(1)}, u32[]{:S(2)}, u32[]{:S(2)}) %collective-permute-start.6) | collective-permute-done | bytes 393248 | tf_op jit(solution)/shard_map/ppermute | solution.py:23
  168.1 14.1 %multiply_reduce_fusion.1 = f32[48,16,128]{2,1,0:T(8,128)S(1)} fusion(f32[48,48,128]{2,1,0:T(8,128)S(1)} %pad_maximum_fusion, f32[48,128]{1,0:T(8,128)S(1)} %copy-done.9, s32[48,16,128]{2,1,0:T(8,128)S(1)} %get-tuple-element.8, f32[48,128]{1,0:T(8,128)S(1)} %copy-done.10, s32[48,16,128]{2,1,0:T(8,128)S(1)} %get-tuple-element.9, f32[48,128]{1,0:T(8,128)S(1)} %copy-done.8, ...), kind=kLoop, calls=%fused_computation.1 | loop fusion | flops 61243392 | bytes 3244032 | tf_op jit(solution)/shard_map/reduce_sum | solution.py:60
  182.2 3.5 collective-permute-start.8
  185.7 2.4 collective-permute-start.9
  189.0 2.9 collective-permute-done.9
  192.4 1.4 copy.83
  194.0 1.0 copy-done
  195.0 5.1 %convolution_bitcast_fusion = f32[48,16,128]{0,1,2:T(8,128)S(1)} fusion(f32[48,64,128]{1,0,2:T(8,128)S(1)} %bitcast.166, f32[8,16,128]{0,1,2:T(8,128)S(1)} %copy.85, f32[48,16,128]{0,1,2:T(8,128)S(1)} %copy.84, f32[8,16,128]{0,1,2:T(8,128)S(1)} %copy-done), kind=kOutput, calls=%fused_computation.7 | convolution fusion | flops 75759616 | bytes 2490368 | tf_op jit(solution)/shard_map/jpc,pic->jic/dot_general | solution.py:78
  200.6 1.9 collective-permute-start.10
  202.5 10.8 %collective-permute-done.10 = f32[48,16,128]{2,1,0:T(8,128)S(1)} collective-permute-done((f32[48,16,128]{2,1,0:T(8,128)S(1)}, f32[48,16,128]{2,1,0:T(8,128)S(1)}, u32[]{:S(2)}, u32[]{:S(2)}) %collective-permute-start.10) | collective-permute-done | bytes 393248 | tf_op jit(solution)/shard_map/ppermute | solution.py:12
  213.9 0.9 broadcast_select_fusion
  215.3 1.9 collective-permute-start.11
  217.2 11.4 %collective-permute-done.11 = f32[48,16,128]{2,1,0:T(8,128)S(1)} collective-permute-done((f32[48,16,128]{2,1,0:T(8,128)S(1)}, f32[48,16,128]{2,1,0:T(8,128)S(1)}, u32[]{:S(2)}, u32[]{:S(2)}) %collective-permute-start.11) | collective-permute-done | bytes 393248 | tf_op jit(solution)/shard_map/ppermute | solution.py:12
  229.2 0.9 broadcast_select_fusion.2
  230.6 2.1 collective-permute-start.12
  232.7 23.8 %collective-permute-done.12 = f32[48,16,128]{2,1,0:T(8,128)S(1)} collective-permute-done((f32[48,16,128]{2,1,0:T(8,128)S(1)}, f32[48,16,128]{2,1,0:T(8,128)S(1)}, u32[]{:S(2)}, u32[]{:S(2)}) %collective-permute-start.12) | collective-permute-done | bytes 393248 | tf_op jit(solution)/shard_map/ppermute | solution.py:12
  257.0 0.9 broadcast_select_fusion.4
  258.4 1.9 collective-permute-start.13
  260.4 23.5 %collective-permute-done.13 = f32[48,16,128]{2,1,0:T(8,128)S(1)} collective-permute-done((f32[48,16,128]{2,1,0:T(8,128)S(1)}, f32[48,16,128]{2,1,0:T(8,128)S(1)}, u32[]{:S(2)}, u32[]{:S(2)}) %collective-permute-start.13) | collective-permute-done | bytes 393248 | tf_op jit(solution)/shard_map/ppermute | solution.py:12
  284.5 0.9 broadcast_select_fusion.6
  285.9 5.1 %collective-permute-start.14 = (f32[48,16,128]{2,1,0:T(8,128)S(1)}, f32[48,16,128]{2,1,0:T(8,128)S(1)}, u32[]{:S(2)}, u32[]{:S(2)}) collective-permute-start(f32[48,16,128]{2,1,0:T(8,128)S(1)} %copy.94), channel_id=1, source_target_pairs={{0,16},{1,17},{2,18},{3,19},{4,20},{5,21},{6,22},{7,23},{8,24},{9,... | collective-permute-start | bytes 1179656 | tf_op jit(solution)/shard_map/ppermute | solution.py:12
  291.0 37.9 %collective-permute-done.14 = f32[48,16,128]{2,1,0:T(8,128)S(1)} collective-permute-done((f32[48,16,128]{2,1,0:T(8,128)S(1)}, f32[48,16,128]{2,1,0:T(8,128)S(1)}, u32[]{:S(2)}, u32[]{:S(2)}) %collective-permute-start.14) | collective-permute-done | bytes 393248 | tf_op jit(solution)/shard_map/ppermute | solution.py:12
  329.5 0.9 broadcast_select_fusion.8
  330.9 1.9 collective-permute-start.15
  332.8 12.5 %collective-permute-done.15 = f32[48,16,128]{2,1,0:T(8,128)S(1)} collective-permute-done((f32[48,16,128]{2,1,0:T(8,128)S(1)}, f32[48,16,128]{2,1,0:T(8,128)S(1)}, u32[]{:S(2)}, u32[]{:S(2)}) %collective-permute-start.15) | collective-permute-done | bytes 393248 | tf_op jit(solution)/shard_map/ppermute | solution.py:12
  346.6 1.9 collective-permute-start.17
  348.6 2.4 collective-permute-start.16
  351.0 2.9 collective-permute-done.17
  353.8 7.4 %collective-permute-done.16 = f32[48,16,128]{2,1,0:T(8,128)S(1)} collective-permute-done((f32[48,16,128]{2,1,0:T(8,128)S(1)}, f32[48,16,128]{2,1,0:T(8,128)S(1)}, u32[]{:S(2)}, u32[]{:S(2)}) %collective-permute-start.16) | collective-permute-done | bytes 393248 | tf_op jit(solution)/shard_map/ppermute | solution.py:23
  361.4 15.8 %multiply_reduce_fusion = f32[48,16,128]{2,1,0:T(8,128)} fusion(f32[48,48,128]{2,1,0:T(8,128)S(1)} %pad_maximum_fusion.1, f32[48,128]{1,0:T(8,128)} %copy.67, s32[48,16,128]{2,1,0:T(8,128)S(1)} %copy-done.2, f32[48,128]{1,0:T(8,128)} %copy.66, s32[48,16,128]{2,1,0:T(8,128)S(1)} %copy-done.4, f32[48,128]{1,0:T(8,128)} %copy.65, s32[48,16,128]{2,1,0:T(8,128)S(1)} %copy-done.6, ...), kind=kLoop, calls=%fused_computation | loop fusion | flops 61243392 | bytes 3244032 | tf_op jit(solution)/shard_map/reduce_sum | solution.py:60
  (100 shorter events, 20.6 us)
Async XLA Ops:
  0.0 19.0 %collective-permute-start = (f32[48,16,128]{2,1,0:T(8,128)}, f32[48,16,128]{2,1,0:T(8,128)S(1)}, u32[]{:S(2)}, u32[]{:S(2)}) collective-permute-start(f32[48,16,128]{2,1,0:T(8,128)} %param.5), channel_id=1, source_target_pairs={{0,1},{1,2},{2,3},{3,4},{4,5},{5,6},{6,7},{7,8},{8,9},{9,10},{10,1... | collective-permute-start | bytes 1179656 | tf_op jit(solution)/shard_map/ppermute | solution.py:12
  4.3 29.8 %copy-start.15 = (pred[48,128]{0,1:T(8,128)(4,1)}, pred[48,128]{0,1:T(8,128)(4,1)S(1)}, u32[]{:S(2)}) copy-start(pred[48,128]{0,1:T(8,128)(4,1)S(1)} %get-tuple-element.30) | copy-start | bytes 18436
  4.3 29.8 %copy-start.14 = (pred[48,128]{0,1:T(8,128)(4,1)}, pred[48,128]{0,1:T(8,128)(4,1)S(1)}, u32[]{:S(2)}) copy-start(pred[48,128]{0,1:T(8,128)(4,1)S(1)} %get-tuple-element.27) | copy-start | bytes 18436
  4.3 50.6 %copy-start.13 = (pred[48,128]{0,1:T(8,128)(4,1)}, pred[48,128]{0,1:T(8,128)(4,1)S(1)}, u32[]{:S(2)}) copy-start(pred[48,128]{0,1:T(8,128)(4,1)S(1)} %get-tuple-element.29) | copy-start | bytes 18436
  4.3 90.4 %copy-start.12 = (pred[48,128]{0,1:T(8,128)(4,1)}, pred[48,128]{0,1:T(8,128)(4,1)S(1)}, u32[]{:S(2)}) copy-start(pred[48,128]{0,1:T(8,128)(4,1)S(1)} %get-tuple-element.28) | copy-start | bytes 18436
  4.3 135.9 %copy-start.11 = (pred[48,128]{0,1:T(8,128)(4,1)}, pred[48,128]{0,1:T(8,128)(4,1)S(1)}, u32[]{:S(2)}) copy-start(pred[48,128]{0,1:T(8,128)(4,1)S(1)} %get-tuple-element.26) | copy-start | bytes 18436
  20.2 13.3 %collective-permute-start.1 = (f32[48,16,128]{2,1,0:T(8,128)S(1)}, f32[48,16,128]{2,1,0:T(8,128)S(1)}, u32[]{:S(2)}, u32[]{:S(2)}) collective-permute-start(f32[48,16,128]{2,1,0:T(8,128)S(1)} %copy.70), channel_id=1, source_target_pairs={{0,2},{1,3},{2,4},{3,5},{4,6},{5,7},{6,8},{7,9},{8,10},{9,11},{10,... | collective-permute-start | bytes 1179656 | tf_op jit(solution)/shard_map/ppermute | solution.py:12
  34.8 19.5 %collective-permute-start.2 = (f32[48,16,128]{2,1,0:T(8,128)S(1)}, f32[48,16,128]{2,1,0:T(8,128)S(1)}, u32[]{:S(2)}, u32[]{:S(2)}) collective-permute-start(f32[48,16,128]{2,1,0:T(8,128)S(1)} %copy.72), channel_id=1, source_target_pairs={{0,4},{1,5},{2,6},{3,7},{4,8},{5,9},{6,10},{7,11},{8,12},{9,13},{1... | collective-permute-start | bytes 1179656 | tf_op jit(solution)/shard_map/ppermute | solution.py:12
  55.6 38.5 %collective-permute-start.3 = (f32[48,16,128]{2,1,0:T(8,128)S(1)}, f32[48,16,128]{2,1,0:T(8,128)S(1)}, u32[]{:S(2)}, u32[]{:S(2)}) collective-permute-start(f32[48,16,128]{2,1,0:T(8,128)S(1)} %copy.74), channel_id=1, source_target_pairs={{0,8},{1,9},{2,10},{3,11},{4,12},{5,13},{6,14},{7,15},{8,16},{9,17... | collective-permute-start | bytes 1179656 | tf_op jit(solution)/shard_map/ppermute | solution.py:12
  95.4 48.6 %copy-start.20 = (f32[4,48,4]{1,2,0:T(4,128)S(1)}, f32[4,48,4]{1,2,0:T(4,128)}, u32[]{:S(2)}) copy-start(f32[4,48,4]{1,2,0:T(4,128)} %param.7) | copy-start | bytes 9220
  95.4 52.1 %copy-start.22 = (s32[48,4]{0,1:T(4,128)S(1)}, s32[48,4]{0,1:T(4,128)}, u32[]{:S(2)}) copy-start(s32[48,4]{0,1:T(4,128)} %param.8) | copy-start | bytes 2308
  95.4 44.2 %collective-permute-start.4 = (f32[48,16,128]{2,1,0:T(8,128)S(1)}, f32[48,16,128]{2,1,0:T(8,128)S(1)}, u32[]{:S(2)}, u32[]{:S(2)}) collective-permute-start(f32[48,16,128]{2,1,0:T(8,128)S(1)} %copy.76), channel_id=1, source_target_pairs={{0,16},{1,17},{2,18},{3,19},{4,20},{5,21},{6,22},{7,23},{8,24},{9,... | collective-permute-start | bytes 1179656 | tf_op jit(solution)/shard_map/ppermute | solution.py:12
  140.9 11.2 %collective-permute-start.5 = (f32[48,16,128]{2,1,0:T(8,128)S(1)}, f32[48,16,128]{2,1,0:T(8,128)S(1)}, u32[]{:S(2)}, u32[]{:S(2)}) collective-permute-start(f32[48,16,128]{2,1,0:T(8,128)S(1)} %copy.78), channel_id=1, source_target_pairs={{0,32},{1,33},{2,34},{3,35},{4,36},{5,37},{6,38},{7,39},{8,40},{9,... | collective-permute-start | bytes 1179656 | tf_op jit(solution)/shard_map/ppermute | solution.py:12
  146.1 11.8 %copy-start.21 = (f32[4,48,4]{1,2,0:T(4,128)S(1)}, f32[4,48,4]{1,2,0:T(4,128)}, u32[]{:S(2)}) copy-start(f32[4,48,4]{1,2,0:T(4,128)} %param.9) | copy-start | bytes 9220
  152.8 15.3 %copy-start.7 = (f32[48,128]{1,0:T(8,128)S(1)}, f32[48,128]{1,0:T(8,128)}, u32[]{:S(2)}) copy-start(f32[48,128]{1,0:T(8,128)} %copy.64) | copy-start | bytes 73732
  152.8 15.3 %copy-start.8 = (f32[48,128]{1,0:T(8,128)S(1)}, f32[48,128]{1,0:T(8,128)}, u32[]{:S(2)}) copy-start(f32[48,128]{1,0:T(8,128)} %copy.65) | copy-start | bytes 73732
  152.8 15.3 %copy-start.9 = (f32[48,128]{1,0:T(8,128)S(1)}, f32[48,128]{1,0:T(8,128)}, u32[]{:S(2)}) copy-start(f32[48,128]{1,0:T(8,128)} %copy.67) | copy-start | bytes 73732
  152.8 15.3 %copy-start.10 = (f32[48,128]{1,0:T(8,128)S(1)}, f32[48,128]{1,0:T(8,128)}, u32[]{:S(2)}) copy-start(f32[48,128]{1,0:T(8,128)} %copy.66) | copy-start | bytes 73732
  153.4 7.2 %collective-permute-start.7 = (f32[48,16,128]{2,1,0:T(8,128)S(1)}, f32[48,16,128]{2,1,0:T(8,128)S(1)}, u32[]{:S(2)}, u32[]{:S(2)}) collective-permute-start(f32[48,16,128]{2,1,0:T(8,128)S(1)} %copy.80), channel_id=1, source_target_pairs={{1,0},{2,1},{3,2},{4,3},{5,4},{6,5},{7,6},{8,7},{9,8},{10,9},{11,1... | collective-permute-start | bytes 1179656 | tf_op jit(solution)/shard_map/ppermute | solution.py:25
  155.3 12.7 %collective-permute-start.6 = (f32[48,16,128]{2,1,0:T(8,128)S(1)}, f32[48,16,128]{2,1,0:T(8,128)S(1)}, u32[]{:S(2)}, u32[]{:S(2)}) collective-permute-start(f32[48,16,128]{2,1,0:T(8,128)S(1)} %copy.80), channel_id=1, source_target_pairs={{0,1},{1,2},{2,3},{3,4},{4,5},{5,6},{6,7},{7,8},{8,9},{9,10},{10,1... | collective-permute-start | bytes 1179656 | tf_op jit(solution)/shard_map/ppermute | solution.py:23
  158.8 29.3 %copy-start.1 = (s32[48,16,128]{2,1,0:T(8,128)}, s32[48,16,128]{2,1,0:T(8,128)S(1)}, u32[]{:S(2)}) copy-start(s32[48,16,128]{2,1,0:T(8,128)S(1)} %get-tuple-element.8) | copy-start | bytes 1179652
  158.8 29.3 %copy-start.3 = (s32[48,16,128]{2,1,0:T(8,128)}, s32[48,16,128]{2,1,0:T(8,128)S(1)}, u32[]{:S(2)}) copy-start(s32[48,16,128]{2,1,0:T(8,128)S(1)} %get-tuple-element.9) | copy-start | bytes 1179652
  158.8 29.3 %copy-start.5 = (s32[48,16,128]{2,1,0:T(8,128)}, s32[48,16,128]{2,1,0:T(8,128)S(1)}, u32[]{:S(2)}) copy-start(s32[48,16,128]{2,1,0:T(8,128)S(1)} %get-tuple-element.10) | copy-start | bytes 1179652
  158.8 29.3 %copy-start.16 = (s32[48,4]{0,1:T(4,128)S(1)}, s32[48,4]{0,1:T(4,128)}, u32[]{:S(2)}) copy-start(s32[48,4]{0,1:T(4,128)} %get-tuple-element.19) | copy-start | bytes 2308
  158.8 29.3 %copy-start.17 = (s32[48,4]{0,1:T(4,128)S(1)}, s32[48,4]{0,1:T(4,128)}, u32[]{:S(2)}) copy-start(s32[48,4]{0,1:T(4,128)} %get-tuple-element.20) | copy-start | bytes 2308
  158.8 29.3 %copy-start.18 = (s32[48,4]{0,1:T(4,128)S(1)}, s32[48,4]{0,1:T(4,128)}, u32[]{:S(2)}) copy-start(s32[48,4]{0,1:T(4,128)} %get-tuple-element.21) | copy-start | bytes 2308
  158.8 29.3 %copy-start.19 = (s32[48,4]{0,1:T(4,128)S(1)}, s32[48,4]{0,1:T(4,128)}, u32[]{:S(2)}) copy-start(s32[48,4]{0,1:T(4,128)} %get-tuple-element.22) | copy-start | bytes 2308
  182.2 10.2 %collective-permute-start.8 = (f32[8,16,128]{2,1,0:T(8,128)S(1)}, f32[8,16,128]{2,1,0:T(8,128)S(1)}, u32[]{:S(2)}, u32[]{:S(2)}) collective-permute-start(f32[8,16,128]{2,1,0:T(8,128)S(1)} %get-tuple-element.5), channel_id=1, source_target_pairs={{0,64},{64,128},{128,192},{192,256},{256,320},{320,384},{384,448},... | collective-permute-start | bytes 196616 | tf_op jit(solution)/shard_map/ppermute | solution.py:23
  185.7 6.2 %collective-permute-start.9 = (f32[8,16,128]{2,1,0:T(8,128)S(1)}, f32[8,16,128]{2,1,0:T(8,128)S(1)}, u32[]{:S(2)}, u32[]{:S(2)}) collective-permute-start(f32[8,16,128]{2,1,0:T(8,128)S(1)} %get-tuple-element.6), channel_id=1, source_target_pairs={{64,0},{128,64},{192,128},{256,192},{320,256},{384,320},{448,384},... | collective-permute-start | bytes 196616 | tf_op jit(solution)/shard_map/ppermute | solution.py:25
  193.8 1.2 copy-start
  200.6 12.7 %collective-permute-start.10 = (f32[48,16,128]{2,1,0:T(8,128)S(1)}, f32[48,16,128]{2,1,0:T(8,128)S(1)}, u32[]{:S(2)}, u32[]{:S(2)}) collective-permute-start(f32[48,16,128]{2,1,0:T(8,128)S(1)} %copy.86), channel_id=1, source_target_pairs={{0,1},{1,2},{2,3},{3,4},{4,5},{5,6},{6,7},{7,8},{8,9},{9,10},{10,1... | collective-permute-start | bytes 1179656 | tf_op jit(solution)/shard_map/ppermute | solution.py:12
  215.3 13.3 %collective-permute-start.11 = (f32[48,16,128]{2,1,0:T(8,128)S(1)}, f32[48,16,128]{2,1,0:T(8,128)S(1)}, u32[]{:S(2)}, u32[]{:S(2)}) collective-permute-start(f32[48,16,128]{2,1,0:T(8,128)S(1)} %copy.88), channel_id=1, source_target_pairs={{0,2},{1,3},{2,4},{3,5},{4,6},{5,7},{6,8},{7,9},{8,10},{9,11},{10,... | collective-permute-start | bytes 1179656 | tf_op jit(solution)/shard_map/ppermute | solution.py:12
  230.6 25.9 %collective-permute-start.12 = (f32[48,16,128]{2,1,0:T(8,128)S(1)}, f32[48,16,128]{2,1,0:T(8,128)S(1)}, u32[]{:S(2)}, u32[]{:S(2)}) collective-permute-start(f32[48,16,128]{2,1,0:T(8,128)S(1)} %copy.90), channel_id=1, source_target_pairs={{0,4},{1,5},{2,6},{3,7},{4,8},{5,9},{6,10},{7,11},{8,12},{9,13},{1... | collective-permute-start | bytes 1179656 | tf_op jit(solution)/shard_map/ppermute | solution.py:12
  258.4 25.5 %collective-permute-start.13 = (f32[48,16,128]{2,1,0:T(8,128)S(1)}, f32[48,16,128]{2,1,0:T(8,128)S(1)}, u32[]{:S(2)}, u32[]{:S(2)}) collective-permute-start(f32[48,16,128]{2,1,0:T(8,128)S(1)} %copy.92), channel_id=1, source_target_pairs={{0,8},{1,9},{2,10},{3,11},{4,12},{5,13},{6,14},{7,15},{8,16},{9,17... | collective-permute-start | bytes 1179656 | tf_op jit(solution)/shard_map/ppermute | solution.py:12
  285.9 43.1 %collective-permute-start.14 = (f32[48,16,128]{2,1,0:T(8,128)S(1)}, f32[48,16,128]{2,1,0:T(8,128)S(1)}, u32[]{:S(2)}, u32[]{:S(2)}) collective-permute-start(f32[48,16,128]{2,1,0:T(8,128)S(1)} %copy.94), channel_id=1, source_target_pairs={{0,16},{1,17},{2,18},{3,19},{4,20},{5,21},{6,22},{7,23},{8,24},{9,... | collective-permute-start | bytes 1179656 | tf_op jit(solution)/shard_map/ppermute | solution.py:12
  330.9 14.4 %collective-permute-start.15 = (f32[48,16,128]{2,1,0:T(8,128)S(1)}, f32[48,16,128]{2,1,0:T(8,128)S(1)}, u32[]{:S(2)}, u32[]{:S(2)}) collective-permute-start(f32[48,16,128]{2,1,0:T(8,128)S(1)} %copy.96), channel_id=1, source_target_pairs={{0,32},{1,33},{2,34},{3,35},{4,36},{5,37},{6,38},{7,39},{8,40},{9,... | collective-permute-start | bytes 1179656 | tf_op jit(solution)/shard_map/ppermute | solution.py:12
  346.1 15.3 %copy-start.2 = (s32[48,16,128]{2,1,0:T(8,128)S(1)}, s32[48,16,128]{2,1,0:T(8,128)}, u32[]{:S(2)}) copy-start(s32[48,16,128]{2,1,0:T(8,128)} %copy-done.1) | copy-start | bytes 1179652
  346.1 15.3 %copy-start.4 = (s32[48,16,128]{2,1,0:T(8,128)S(1)}, s32[48,16,128]{2,1,0:T(8,128)}, u32[]{:S(2)}) copy-start(s32[48,16,128]{2,1,0:T(8,128)} %copy-done.3) | copy-start | bytes 1179652
  346.1 15.3 %copy-start.6 = (s32[48,16,128]{2,1,0:T(8,128)S(1)}, s32[48,16,128]{2,1,0:T(8,128)}, u32[]{:S(2)}) copy-start(s32[48,16,128]{2,1,0:T(8,128)} %copy-done.5) | copy-start | bytes 1179652
  346.6 7.2 %collective-permute-start.17 = (f32[48,16,128]{2,1,0:T(8,128)S(1)}, f32[48,16,128]{2,1,0:T(8,128)S(1)}, u32[]{:S(2)}, u32[]{:S(2)}) collective-permute-start(f32[48,16,128]{2,1,0:T(8,128)S(1)} %copy.98), channel_id=1, source_target_pairs={{1,0},{2,1},{3,2},{4,3},{5,4},{6,5},{7,6},{8,7},{9,8},{10,9},{11,1... | collective-permute-start | bytes 1179656 | tf_op jit(solution)/shard_map/ppermute | solution.py:25
  348.6 12.7 %collective-permute-start.16 = (f32[48,16,128]{2,1,0:T(8,128)S(1)}, f32[48,16,128]{2,1,0:T(8,128)S(1)}, u32[]{:S(2)}, u32[]{:S(2)}) collective-permute-start(f32[48,16,128]{2,1,0:T(8,128)S(1)} %copy.98), channel_id=1, source_target_pairs={{0,1},{1,2},{2,3},{3,4},{4,5},{5,6},{6,7},{7,8},{8,9},{9,10},{10,1... | collective-permute-start | bytes 1179656 | tf_op jit(solution)/shard_map/ppermute | solution.py:23
where the time goes:
time: 378 us; the launch traced here: 377 us
  waiting for transfers between devices  269 us (71%)
  starting transfers between devices  42.3 us (11%)
  other arithmetic  38.1 us (10%)
  local copies, waits for them, and re-layouts  22.2 us (6%)
  matrix products  5.06 us (1%)
    ppermute x12, waiting for transfers between devices, passed_along(): return lax.ppermute(value, axis, pairs)  246 us
    reduce_sum x2, other arithmetic, zonal_pass(): return jnp.sum(banded * extended[:, None, :, :], axis=2)  29.9 us
    ppermute x12, starting transfers between devices, passed_along(): return lax.ppermute(value, axis, pairs)  27.6 us
    ppermute x3, waiting for transfers between devices, extended_2(): lax.ppermute(tail, axis, [(i, (i + 1) % count) for i in range(ends)])  14.9 us
    ppermute x3, starting transfers between devices, extended_2(): lax.ppermute(tail, axis, [(i, (i + 1) % count) for i in range(ends)])  8.48 us
  transfers between devices with their start and end apart: 18, of which 17 were waited for; matrix products, arithmetic and copies ran while one was open for 2% of the time, Pallas kernels for 0%

commit v1 on v0

v1 whole, which is shorter than its diff:
```python
import functools

import jax
import jax.numpy as jnp
from jax import lax
from jax.experimental import pallas as pl
from jax.experimental.pallas import tpu as pltpu
from jax.sharding import PartitionSpec as P

TMAX = 6
REACH = 8
VMEM = pltpu.VMEM
SMEM = pltpu.SMEM


def turn_kernel(x_ref, o_ref):
    for i in range(x_ref.shape[0] // 128):
        for j in range(x_ref.shape[1] // 128):
            o_ref[j * 128 : (j + 1) * 128, i * 128 : (i + 1) * 128] = x_ref[
                i * 128 : (i + 1) * 128, j * 128 : (j + 1) * 128
            ].T


def turned(x):
    return pl.pallas_call(
        turn_kernel,
        out_shape=jax.ShapeDtypeStruct((x.shape[1], x.shape[0]), x.dtype),
        in_specs=[pl.BlockSpec(memory_space=VMEM)],
        out_specs=pl.BlockSpec(memory_space=VMEM),
        name="turn",
    )(x)


def rotate(line, offset, weights, ext_ref, cells, lanes_per_block):
    lanes = line.shape[1]
    circle = lanes // lanes_per_block * cells
    wrapped = lax.rem(offset + circle, circle)
    step = lax.div(wrapped, cells) * lanes_per_block
    rest = lax.rem(wrapped, cells)
    before = lax.rem(step + lanes_per_block, lanes)
    after = lax.rem(step + lanes - lanes_per_block, lanes)
    ext_ref[0:cells] = pltpu.roll(line, before, 1)
    ext_ref[cells : 2 * cells] = pltpu.roll(line, step, 1)
    ext_ref[2 * cells : 2 * cells + 8] = pltpu.roll(line[0:8], after, 1)
    total = None
    for k in range(4):
        term = weights[k] * ext_ref[pl.ds(cells - 1 - rest + k, cells), :]
        total = term if total is None else total + term
    return total


def first_kernel(cells, per_block, levels, x_ref, off_ref, w_ref, o_ref, turn_ref, ext_ref):
    rows = x_ref.shape[1] // cells
    level = lax.div(lax.axis_index("lon") * levels, lax.axis_size("lon"))
    for i in range(x_ref.shape[1] // 128):
        turn_ref[i * 128 : (i + 1) * 128, :] = x_ref[:, i * 128 : (i + 1) * 128].T
    for r in range(rows):
        weights = [w_ref[k, r, level] for k in range(4)]
        o_ref[r * cells : (r + 1) * cells, :] = rotate(
            turn_ref[r * cells : (r + 1) * cells, :],
            off_ref[r, level],
            weights,
            ext_ref.at[r],
            cells,
            per_block,
        )


def second_kernel(
    cells, per_block, levels, f_ref, lo_ref, hi_ref, off_ref, w_ref, toff_ref, tw_ref, o_ref, all_ref, turn_ref, ext_ref
):
    rows = f_ref.shape[0] // cells
    level = lax.div(lax.axis_index("lon") * levels, lax.axis_size("lon"))
    first_row = lax.axis_index("band") * rows
    last_row = lax.axis_size("band") * rows - 1
    edge = REACH * cells
    all_ref[0:edge] = lo_ref[...]
    all_ref[edge : edge + rows * cells] = f_ref[...]
    all_ref[edge + rows * cells : 2 * edge + rows * cells] = hi_ref[...]
    for r in range(rows):
        shift = toff_ref[r, level]
        total = None
        for k in range(4):
            source = jnp.clip(first_row + r - shift + (k - 1), 0, last_row) - first_row + REACH
            term = tw_ref[k, r, level] * all_ref[pl.ds(pl.multiple_of(source * cells, cells), cells), :]
            total = term if total is None else total + term
        weights = [w_ref[k, r, level] for k in range(4)]
        turn_ref[r * cells : (r + 1) * cells, :] = rotate(
            total, off_ref[r, level], weights, ext_ref.at[r], cells, per_block
        )
    for i in range(o_ref.shape[1] // 128):
        o_ref[:, i * 128 : (i + 1) * 128] = turn_ref[i * 128 : (i + 1) * 128, :].T


def spread(x, groups):
    n, m = x.shape
    y = lax.all_to_all(x.reshape(groups, n // groups, m), "lon", 0, 0, tiled=True)
    return y.reshape(n, m)


def per_device(tracers, lon_offset, lon_weights, lat_offset, lat_weights):
    rows, cells, columns = tracers.shape
    levels = lon_offset.shape[1]
    groups = lax.axis_size("lon")
    per_block = columns // groups
    bands = lax.axis_size("band")
    flat = rows * cells
    edge = REACH * cells
    vspec = pl.BlockSpec(memory_space=VMEM)
    sspec = pl.BlockSpec(memory_space=SMEM)

    gathered = spread(turned(tracers.reshape(flat, columns)), groups)
    first = pl.pallas_call(
        functools.partial(first_kernel, cells, per_block, levels),
        out_shape=jax.ShapeDtypeStruct((flat, columns), jnp.float32),
        in_specs=[vspec, sspec, sspec],
        out_specs=vspec,
        scratch_shapes=[VMEM((flat, columns), jnp.float32), VMEM((rows, 2 * cells + 8, columns), jnp.float32)],
        name="first",
    )(gathered, lon_offset, lon_weights)
    lo = lax.ppermute(first[flat - edge :], "band", [(i, i + 1) for i in range(bands - 1)])
    hi = lax.ppermute(first[:edge], "band", [(i + 1, i) for i in range(bands - 1)])
    out = pl.pallas_call(
        functools.partial(second_kernel, cells, per_block, levels),
        out_shape=jax.ShapeDtypeStruct((columns, flat), jnp.float32),
        in_specs=[vspec, vspec, vspec, sspec, sspec, sspec, sspec],
        out_specs=vspec,
        scratch_shapes=[
            VMEM((flat + 2 * edge, columns), jnp.float32),
            VMEM((flat, columns), jnp.float32),
            VMEM((rows, 2 * cells + 8, columns), jnp.float32),
        ],
        name="second",
    )(first, lo, hi, lon_offset, lon_weights, lat_offset, lat_weights)
    return turned(spread(out, groups)).reshape(rows, cells, columns)


def solution(mesh):
    return jax.shard_map(
        per_device,
        mesh=mesh,
        in_specs=(
            P("band", "lon", None),
            P("band", None),
            P(None, "band", None),
            P("band", None),
            P(None, "band", None),
        ),
        out_specs=P("band", "lon", None),
        check_vma=False,
    )
```

time: 378 us -> 117 us (0.31)
  the two profiles are of different devices: /device:TPU:8 before, /device:TPU:3 now
where the time goes in v1:
time: 117 us; the launch traced here: 116 us
  blocking collectives  34.3 us (29%)
  waiting for transfers between devices  31.4 us (27%)
  starting transfers between devices  25.4 us (22%)
  Pallas kernels  15.3 us (13%)
  local copies, waits for them, and re-layouts  9.65 us (8%)
    all_to_all x1, blocking collectives, spread(): lax.all_to_all(x.reshape(groups, n // groups, m), 'lon', 0, 0, tiled=True)  34.3 us
    all_to_all x1, waiting for transfers between devices, spread(): lax.all_to_all(x.reshape(groups, n // groups, m), 'lon', 0, 0, tiled=True)  27.3 us
    all_to_all x1, starting transfers between devices, spread(): lax.all_to_all(x.reshape(groups, n // groups, m), 'lon', 0, 0, tiled=True)  18 us
    pallas_call x1, Pallas kernels, per_device(): pl.pallas_call(functools.partial(second_kernel, cells, per_block, levels)...  7.04 us
    ppermute x1, starting transfers between devices, per_device(): lax.ppermute(first[:edge], 'band', [(i + 1, i) for i in range(bands - 1)])  5.51 us
    pallas_call x1, Pallas kernels, per_device(): pl.pallas_call(functools.partial(first_kernel, cells, per_block, levels),...  4.49 us
    ppermute x1, waiting for transfers between devices, per_device(): lax.ppermute(first[flat - edge:], 'band', [(i, i + 1) for i in range(band...  4.03 us
    pallas_call x2, Pallas kernels, turned(): pl.pallas_call(turn_kernel, out_shape=jax.ShapeDtypeStruct((x.shape[1], x...  3.82 us
  transfers between devices with their start and end apart: 3, of which 2 were waited for; matrix products, arithmetic and copies ran while one was open for 3% of the time, Pallas kernels for 0%

profile of v1, /device:TPU:3, one launch (start us, length us, event | category | flops | bytes accessed | tf_op | source)
XLA Modules:
  0.0 116.2 jit_solution(6415446940520910502)
XLA Ops:
  0.0 1.9 %turn.2 = f32[128,768]{1,0:T(8,128)} custom-call(f32[768,128]{1,0:T(8,128)} %bitcast.2), custom_call_target="tpu_custom_call" | custom-call | tf_op jit(solution)/shard_map/turn/pallas_call | solution.py:25
  1.9 2.0 %reshape.19 = f32[64,2,768]{2,1,0:T(2,128)} reshape(f32[128,768]{1,0:T(8,128)} %turn.2) | data formatting | bytes 786432 | tf_op jit(solution)/shard_map/reshape | solution.py:97
  3.9 0.0 copy-start.4
  3.9 18.0 %all-to-all-start = ((f32[64,2,768]{2,1,0:T(2,128)}), f32[64,2,768]{2,1,0:T(2,128)S(1)}, u32[]{:S(2)}, u32[]{:S(2)}) async-start(f32[64,2,768]{2,1,0:T(2,128)} %reshape.19), calls=%async_computation | async-start | bytes 786432 | tf_op jit(solution)/shard_map/all_to_all | solution.py:97
  21.9 0.0 copy-done.4
  21.9 0.0 copy-start.2
  21.9 0.7 copy.6.off_ref
  22.6 0.0 copy-done.2
  22.6 0.8 copy.7.w_ref
  23.4 27.3 %all-to-all-done = f32[64,2,768]{2,1,0:T(2,128)S(1)} async-done(((f32[64,2,768]{2,1,0:T(2,128)}), f32[64,2,768]{2,1,0:T(2,128)S(1)}, u32[]{:S(2)}, u32[]{:S(2)}) %all-to-all-start) | async-done | bytes 393248 | tf_op jit(solution)/shard_map/all_to_all | solution.py:97
  50.7 1.0 reshape.20.x_ref
  51.7 4.5 %first.1.f_ref = f32[768,128]{1,0:T(8,128)} custom-call(f32[128,768]{1,0:T(8,128)} %reshape.20.x_ref, s32[48,4]{1,0:T(8,128)} %copy.6.off_ref, f32[4,48,4]{2,1,0:T(8,128)} %copy.7.w_ref), custom_call_target="tpu_custom_call" | custom-call | tf_op jit(solution)/shard_map/first/pallas_call | solution.py:113
  56.2 0.9 fusion
  57.1 0.0 copy-start.5
  57.1 5.5 %collective-permute-start.1 = (f32[128,128]{1,0:T(8,128)S(1)}, f32[128,128]{1,0:T(8,128)S(1)}, u32[]{:S(2)}, u32[]{:S(2)}) collective-permute-start(f32[128,128]{1,0:T(8,128)S(1)} %get-tuple-element.5), channel_id=1, source_target_pairs={{64,0},{128,64},{192,128},{256,192},{320,256},{384,320},{448,384},... | collective-permute-start | bytes 196616 | tf_op jit(solution)/shard_map/ppermute | solution.py:122
  62.6 0.0 copy-start.3
  62.6 1.9 %collective-permute-start = (f32[128,128]{1,0:T(8,128)S(1)}, f32[128,128]{1,0:T(8,128)S(1)}, u32[]{:S(2)}, u32[]{:S(2)}) collective-permute-start(f32[128,128]{1,0:T(8,128)S(1)} %get-tuple-element.6), channel_id=1, source_target_pairs={{0,64},{64,128},{128,192},{192,256},{256,320},{320,384},{384,448},... | collective-permute-start | bytes 196616 | tf_op jit(solution)/shard_map/ppermute | solution.py:121
  64.6 0.0 copy-done.5
  64.6 0.7 copy.10.toff_ref
  65.3 0.0 copy-done.3
  65.3 0.7 copy.11.tw_ref
  66.0 0.0 collective-permute-done.1.hi_ref
  66.0 0.0 copy-start
  66.0 4.0 %collective-permute-done.lo_ref = f32[128,128]{1,0:T(8,128)S(1)} collective-permute-done((f32[128,128]{1,0:T(8,128)S(1)}, f32[128,128]{1,0:T(8,128)S(1)}, u32[]{:S(2)}, u32[]{:S(2)}) %collective-permute-start) | collective-permute-done | bytes 65568 | tf_op jit(solution)/shard_map/ppermute | solution.py:121
  70.1 0.0 copy-done
  70.1 0.0 copy-start.1
  70.1 0.6 copy-done.1
  70.7 7.0 %second.1 = f32[128,768]{1,0:T(8,128)} custom-call(f32[768,128]{1,0:T(8,128)} %first.1.f_ref, f32[128,128]{1,0:T(8,128)} %copy-done.1, f32[128,128]{1,0:T(8,128)} %copy-done, s32[48,4]{1,0:T(8,128)} %copy.6.off_ref, f32[4,48,4]{2,1,0:T(8,128)} %copy.7.w_ref, s32[48,4]{1,0:T(8,128)} %copy.10.toff_ref, f32[4,48,4]{2,1,0:T(8,128)} %copy.11.tw_ref), custom_call_target="tpu_custom_call" | custom-call | tf_op jit(solution)/shard_map/second/pallas_call | solution.py:123
  77.7 1.2 %reshape.21 = f32[64,2,768]{2,1,0:T(2,128)S(1)} reshape(f32[128,768]{1,0:T(8,128)} %second.1) | data formatting | bytes 786432 | tf_op jit(solution)/shard_map/reshape | solution.py:97
  79.0 34.3 %all_to_all.10 = f32[64,2,768]{2,1,0:T(2,128)S(1)} all-to-all(f32[64,2,768]{2,1,0:T(2,128)S(1)} %reshape.21), channel_id=1, replica_groups=mesh['band'=8,'lon'=64] {'lon'}, dimensions={0} | all-to-all | bytes 786432 | tf_op jit(solution)/shard_map/all_to_all | solution.py:97
  113.3 1.0 reshape.22.x_ref
  114.3 1.9 %turn.3 = f32[768,128]{1,0:T(8,128)} custom-call(f32[128,768]{1,0:T(8,128)} %reshape.22.x_ref), custom_call_target="tpu_custom_call" | custom-call | tf_op jit(solution)/shard_map/turn/pallas_call | solution.py:25
Async XLA Ops:
  3.9 18.0 %copy-start.4 = (s32[48,4]{0,1:T(4,128)S(1)}, s32[48,4]{0,1:T(4,128)}, u32[]{:S(2)}) copy-start(s32[48,4]{0,1:T(4,128)} %param.6) | copy-start | bytes 2308
  3.9 46.8 %all-to-all-start = ((f32[64,2,768]{2,1,0:T(2,128)}), f32[64,2,768]{2,1,0:T(2,128)S(1)}, u32[]{:S(2)}, u32[]{:S(2)}) async-start(f32[64,2,768]{2,1,0:T(2,128)} %reshape.19), calls=%async_computation | async-start | bytes 786432 | tf_op jit(solution)/shard_map/all_to_all | solution.py:97
  21.9 0.7 copy-start.2
  57.1 7.5 %copy-start.5 = (s32[48,4]{0,1:T(4,128)S(1)}, s32[48,4]{0,1:T(4,128)}, u32[]{:S(2)}) copy-start(s32[48,4]{0,1:T(4,128)} %param.8) | copy-start | bytes 2308
  57.1 8.9 %collective-permute-start.1 = (f32[128,128]{1,0:T(8,128)S(1)}, f32[128,128]{1,0:T(8,128)S(1)}, u32[]{:S(2)}, u32[]{:S(2)}) collective-permute-start(f32[128,128]{1,0:T(8,128)S(1)} %get-tuple-element.5), channel_id=1, source_target_pairs={{64,0},{128,64},{192,128},{256,192},{320,256},{384,320},{448,384},... | collective-permute-start | bytes 196616 | tf_op jit(solution)/shard_map/ppermute | solution.py:122
  62.6 2.7 %copy-start.3 = (f32[4,48,4]{1,2,0:T(4,128)S(1)}, f32[4,48,4]{1,2,0:T(4,128)}, u32[]{:S(2)}) copy-start(f32[4,48,4]{1,2,0:T(4,128)} %param.9) | copy-start | bytes 9220
  62.6 7.4 %collective-permute-start = (f32[128,128]{1,0:T(8,128)S(1)}, f32[128,128]{1,0:T(8,128)S(1)}, u32[]{:S(2)}, u32[]{:S(2)}) collective-permute-start(f32[128,128]{1,0:T(8,128)S(1)} %get-tuple-element.6), channel_id=1, source_target_pairs={{0,64},{64,128},{128,192},{192,256},{256,320},{320,384},{384,448},... | collective-permute-start | bytes 196616 | tf_op jit(solution)/shard_map/ppermute | solution.py:121
  66.0 4.0 %copy-start = (f32[128,128]{1,0:T(8,128)}, f32[128,128]{1,0:T(8,128)S(1)}, u32[]{:S(2)}) copy-start(f32[128,128]{1,0:T(8,128)S(1)} %collective-permute-done.1.hi_ref) | copy-start | bytes 196612
  70.1 0.6 copy-start.1

commit v2 on v1

v2 whole, which is shorter than its diff:
```python
import functools

import jax
import jax.numpy as jnp
from jax import lax
from jax.experimental import pallas as pl
from jax.experimental.pallas import tpu as pltpu
from jax.sharding import PartitionSpec as P

TMAX = 6
REACH = 8
VMEM = pltpu.VMEM
SMEM = pltpu.SMEM
PARAMS = pltpu.CompilerParams(vmem_limit_bytes=8 * 1024 * 1024)


def turn_kernel(x_ref, o_ref):
    for i in range(x_ref.shape[0] // 128):
        for j in range(x_ref.shape[1] // 128):
            o_ref[j * 128 : (j + 1) * 128, i * 128 : (i + 1) * 128] = x_ref[
                i * 128 : (i + 1) * 128, j * 128 : (j + 1) * 128
            ].T


def turned(x):
    return pl.pallas_call(
        turn_kernel,
        out_shape=jax.ShapeDtypeStruct((x.shape[1], x.shape[0]), x.dtype),
        in_specs=[pl.BlockSpec(memory_space=VMEM)],
        out_specs=pl.BlockSpec(memory_space=VMEM),
        compiler_params=PARAMS,
        name="turn",
    )(x)


def rotate(line, offset, weights, ext_ref, cells, lanes_per_block):
    lanes = line.shape[1]
    circle = lanes // lanes_per_block * cells
    wrapped = offset & (circle - 1)
    rest = wrapped & (cells - 1)
    step = (wrapped >> (cells.bit_length() - 1)) * lanes_per_block
    before = (step + lanes_per_block) & (lanes - 1)
    after = (step + lanes - lanes_per_block) & (lanes - 1)
    ext_ref[0:cells] = pltpu.roll(line, before, 1)
    ext_ref[cells : 2 * cells] = pltpu.roll(line, step, 1)
    ext_ref[2 * cells : 2 * cells + 8] = pltpu.roll(line[0:8], after, 1)
    total = None
    for k in range(4):
        term = weights[k] * ext_ref[pl.ds(cells - 1 - rest + k, cells), :]
        total = term if total is None else total + term
    return total


def first_kernel(cells, per_block, levels, x_ref, off_ref, w_ref, o_ref, head_ref, tail_ref, turn_ref, ext_ref):
    rows = x_ref.shape[1] // cells
    level = lax.div(lax.axis_index("lon") * levels, lax.axis_size("lon"))
    for i in range(x_ref.shape[1] // 128):
        turn_ref[i * 128 : (i + 1) * 128, :] = x_ref[:, i * 128 : (i + 1) * 128].T
    for r in range(rows):
        value = rotate(
            turn_ref[r * cells : (r + 1) * cells, :],
            off_ref[level, r],
            [w_ref[k, level, r] for k in range(4)],
            ext_ref.at[r],
            cells,
            per_block,
        )
        o_ref[r * cells : (r + 1) * cells, :] = value
        if r < REACH:
            head_ref[r * cells : (r + 1) * cells, :] = value
        if r >= rows - REACH:
            s = r - (rows - REACH)
            tail_ref[s * cells : (s + 1) * cells, :] = value


def rows_done(chosen, rows, cells, per_block, levels, source_ref, first_place, scalars, o_ref, turn_ref, ext_ref):
    off_ref, w_ref, toff_ref, tw_ref = scalars
    level = lax.div(lax.axis_index("lon") * levels, lax.axis_size("lon"))
    first_row = lax.axis_index("band") * rows
    last_row = lax.axis_size("band") * rows - 1
    for r in chosen:
        shift = toff_ref[level, r]
        total = None
        for k in range(4):
            source = jnp.clip(first_row + (r + k - 1) - shift, 0, last_row) - first_row - first_place
            term = tw_ref[k, level, r] * source_ref[pl.ds(pl.multiple_of(source * cells, cells), cells), :]
            total = term if total is None else total + term
        turn_ref[r * cells : (r + 1) * cells, :] = rotate(
            total, off_ref[level, r], [w_ref[k, level, r] for k in range(4)], ext_ref.at[r], cells, per_block
        )
    per_turn = 128 // cells
    for i in sorted({r // per_turn for r in chosen}):
        o_ref[:, i * 128 : (i + 1) * 128] = turn_ref[i * 128 : (i + 1) * 128, :].T


def inner_kernel(cells, per_block, levels, f_ref, off_ref, w_ref, toff_ref, tw_ref, o_ref, turn_ref, ext_ref):
    rows = f_ref.shape[0] // cells
    scalars = (off_ref, w_ref, toff_ref, tw_ref)
    chosen = range(REACH, rows - REACH)
    rows_done(chosen, rows, cells, per_block, levels, f_ref, 0, scalars, o_ref, turn_ref, ext_ref)


def outer_kernel(
    cells, per_block, levels, f_ref, lo_ref, hi_ref, off_ref, w_ref, toff_ref, tw_ref, i_ref, o_ref, all_ref, turn_ref, ext_ref
):
    rows = f_ref.shape[0] // cells
    edge = REACH * cells
    flat = rows * cells
    scalars = (off_ref, w_ref, toff_ref, tw_ref)
    all_ref[0:edge] = lo_ref[...]
    all_ref[edge : 3 * edge] = f_ref[0 : 2 * edge]
    all_ref[flat - edge : flat + edge] = f_ref[flat - 2 * edge :]
    all_ref[flat + edge : flat + 2 * edge] = hi_ref[...]
    chosen = [*range(REACH), *range(rows - REACH, rows)]
    rows_done(chosen, rows, cells, per_block, levels, all_ref, -REACH, scalars, o_ref, turn_ref, ext_ref)


def spread(x, groups):
    n, m = x.shape
    y = lax.all_to_all(x.reshape(groups, n // groups, m), "lon", 0, 0, tiled=True)
    return y.reshape(n, m)


def per_device(tracers, lon_offset, lon_weights, lat_offset, lat_weights):
    rows, cells, columns = tracers.shape
    levels = lon_offset.shape[1]
    groups = lax.axis_size("lon")
    per_block = columns // groups
    bands = lax.axis_size("band")
    flat = rows * cells
    edge = REACH * cells
    f32 = jnp.float32
    vspec = pl.BlockSpec(memory_space=VMEM)
    sspec = pl.BlockSpec(memory_space=SMEM)
    scalars = (lon_offset.T, lon_weights.transpose(0, 2, 1), lat_offset.T, lat_weights.transpose(0, 2, 1))
    scratch = [VMEM((flat, columns), f32), VMEM((rows, 2 * cells + 8, columns), f32)]

    gathered = spread(turned(tracers.reshape(flat, columns)), groups)
    first, head, tail = pl.pallas_call(
        functools.partial(first_kernel, cells, per_block, levels),
        out_shape=[jax.ShapeDtypeStruct((n, columns), f32) for n in (flat, edge, edge)],
        in_specs=[vspec, sspec, sspec],
        out_specs=[vspec] * 3,
        scratch_shapes=scratch,
        compiler_params=PARAMS,
        name="first",
    )(gathered, *scalars[:2])
    lo = lax.ppermute(tail, "band", [(i, i + 1) for i in range(bands - 1)])
    hi = lax.ppermute(head, "band", [(i + 1, i) for i in range(bands - 1)])
    inner = pl.pallas_call(
        functools.partial(inner_kernel, cells, per_block, levels),
        out_shape=jax.ShapeDtypeStruct((columns, flat), f32),
        in_specs=[vspec] + [sspec] * 4,
        out_specs=vspec,
        scratch_shapes=scratch,
        compiler_params=PARAMS,
        name="inner",
    )(first, *scalars)
    out = pl.pallas_call(
        functools.partial(outer_kernel, cells, per_block, levels),
        out_shape=jax.ShapeDtypeStruct((columns, flat), f32),
        in_specs=[vspec] * 3 + [sspec] * 4 + [vspec],
        out_specs=vspec,
        scratch_shapes=[VMEM((flat + 2 * edge, columns), f32), *scratch],
        input_output_aliases={7: 0},
        compiler_params=PARAMS,
        name="outer",
    )(first, lo, hi, *scalars, inner)
    return turned(spread(out, groups)).reshape(rows, cells, columns)


def solution(mesh):
    return jax.shard_map(
        per_device,
        mesh=mesh,
        in_specs=(
            P("band", "lon", None),
            P("band", None),
            P(None, "band", None),
            P("band", None),
            P(None, "band", None),
        ),
        out_specs=P("band", "lon", None),
        check_vma=False,
    )
```

time: 117 us -> 98.2 us (0.84)
  the two profiles are of different devices: /device:TPU:3 before, /device:TPU:25 now
where the time goes in v2:
time: 98.2 us; the launch traced here: 97.9 us
  blocking collectives  82.2 us (84%)
  starting transfers between devices  5.28 us (5%)
  Pallas kernels  5.25 us (5%)
  local copies, waits for them, and re-layouts  2.68 us (3%)
  waiting for transfers between devices  2.41 us (2%)
    all_to_all x2, blocking collectives, spread(): lax.all_to_all(x.reshape(groups, n // groups, m), 'lon', 0, 0, tiled=True)  82.2 us
    ppermute x1, starting transfers between devices, per_device(): hi = lax.ppermute(head, 'band', [(i + 1, i) for i in range(bands - 1)])  3.36 us
    ppermute x1, waiting for transfers between devices, per_device(): hi = lax.ppermute(head, 'band', [(i + 1, i) for i in range(bands - 1)])  2.4 us
  transfers between devices with their start and end apart: 2, of which 1 were waited for; matrix products, arithmetic and copies ran while one was open for 0% of the time, Pallas kernels for 2%

profile of v2, /device:TPU:25, one launch (start us, length us, event | category | flops | bytes accessed | tf_op | source)
XLA Modules:
  0.0 97.9 jit_solution(17726839795031231883)
XLA Ops:
  0.0 0.0 copy-start
  0.0 1.0 %copy-done = f32[48,16,128]{2,1,0:T(8,128)S(1)} copy-done((f32[48,16,128]{2,1,0:T(8,128)S(1)}, f32[48,16,128]{2,1,0:T(8,128)}, u32[]{:S(2)}) %copy-start) | copy-done | bytes 393240
  1.0 0.2 turn.2
  1.2 0.2 reshape.19
  1.4 47.4 %all_to_all.10 = f32[64,2,768]{2,1,0:T(2,128)S(1)} all-to-all(f32[64,2,768]{2,1,0:T(2,128)S(1)} %reshape.19), channel_id=1, replica_groups=mesh['band'=8,'lon'=64] {'lon'}, dimensions={0} | all-to-all | bytes 786432 | tf_op jit(solution)/shard_map/all_to_all | solution.py:120
  48.8 0.0 copy-start.1
  48.8 0.3 reshape.20.x_ref
  49.1 0.0 copy-start.3
  49.1 0.4 copy-done.1
  49.5 0.3 copy-done.3
  49.8 0.0 copy-start.4
  49.8 1.3 %first.1 = (f32[768,128]{1,0:T(8,128)S(1)}, f32[128,128]{1,0:T(8,128)S(1)}, f32[128,128]{1,0:T(8,128)S(1)}) custom-call(f32[128,768]{1,0:T(8,128)S(1)} %reshape.20.x_ref, s32[4,48]{1,0:T(4,128)S(1)} %bitcast.12, f32[4,4,48]{2,1,0:T(4,128)S(1)} %bitcast.7), custom_call_target="tpu_custom_call" | custom-call | tf_op jit(solution)/shard_map/first/pallas_call | solution.py:139
  51.1 0.0 copy-start.2
  51.1 1.9 %collective-permute-start = (f32[128,128]{1,0:T(8,128)S(1)}, f32[128,128]{1,0:T(8,128)S(1)}, u32[]{:S(2)}, u32[]{:S(2)}) collective-permute-start(f32[128,128]{1,0:T(8,128)S(1)} %get-tuple-element.9), channel_id=1, source_target_pairs={{0,64},{64,128},{128,192},{192,256},{256,320},{320,384},{384,448},... | collective-permute-start | bytes 196616 | tf_op jit(solution)/shard_map/ppermute | solution.py:148
  53.0 3.4 %collective-permute-start.1 = (f32[128,128]{1,0:T(8,128)S(1)}, f32[128,128]{1,0:T(8,128)S(1)}, u32[]{:S(2)}, u32[]{:S(2)}) collective-permute-start(f32[128,128]{1,0:T(8,128)S(1)} %get-tuple-element.10), channel_id=1, source_target_pairs={{64,0},{128,64},{192,128},{256,192},{320,256},{384,320},{448,384},... | collective-permute-start | bytes 196616 | tf_op jit(solution)/shard_map/ppermute | solution.py:149
  56.4 0.0 copy-done.4
  56.4 0.0 copy-done.2
  56.4 1.6 %inner.1.i_ref = f32[128,768]{1,0:T(8,128)S(1)} custom-call(f32[768,128]{1,0:T(8,128)S(1)} %get-tuple-element.8.f_ref, s32[4,48]{1,0:T(4,128)S(1)} %bitcast.13, f32[4,4,48]{2,1,0:T(4,128)S(1)} %bitcast.8, s32[4,48]{1,0:T(4,128)S(1)} %bitcast.15, f32[4,4,48]{2,1,0:T(4,128)S(1)} %bitcast.10), custom_call_target="tpu_custom_call" | custom-call | tf_op jit(solution)/shard_map/inner/pallas_call | solution.py:150
  58.0 0.0 collective-permute-done.lo_ref
  58.0 2.4 %collective-permute-done.1.hi_ref = f32[128,128]{1,0:T(8,128)S(1)} collective-permute-done((f32[128,128]{1,0:T(8,128)S(1)}, f32[128,128]{1,0:T(8,128)S(1)}, u32[]{:S(2)}, u32[]{:S(2)}) %collective-permute-start.1) | collective-permute-done | bytes 65568 | tf_op jit(solution)/shard_map/ppermute | solution.py:149
  60.4 1.3 %outer.1 = f32[128,768]{1,0:T(8,128)S(1)} custom-call(f32[768,128]{1,0:T(8,128)S(1)} %get-tuple-element.8.f_ref, f32[128,128]{1,0:T(8,128)S(1)} %collective-permute-done.lo_ref, f32[128,128]{1,0:T(8,128)S(1)} %collective-permute-done.1.hi_ref, s32[4,48]{1,0:T(4,128)S(1)} %bitcast.14, f32[4,4,48]{2,1,0:T(4,128)S(1)} %bitcast.9, ...), custom_call_target="tpu_custom_call", output_to_operand_aliasing={{}: (7, {})} | custom-call | tf_op jit(solution)/shard_map/outer/pallas_call | solution.py:159
  61.7 0.2 reshape.21
  61.9 34.8 %all_to_all.11 = f32[64,2,768]{2,1,0:T(2,128)S(1)} all-to-all(f32[64,2,768]{2,1,0:T(2,128)S(1)} %reshape.21), channel_id=1, replica_groups=mesh['band'=8,'lon'=64] {'lon'}, dimensions={0} | all-to-all | bytes 786432 | tf_op jit(solution)/shard_map/all_to_all | solution.py:120
  96.7 0.3 reshape.22.x_ref
  97.0 0.9 turn.3
Async XLA Ops:
  0.0 1.0 %copy-start = (f32[48,16,128]{2,1,0:T(8,128)S(1)}, f32[48,16,128]{2,1,0:T(8,128)}, u32[]{:S(2)}) copy-start(f32[48,16,128]{2,1,0:T(8,128)} %param.5) | copy-start | bytes 1179652
  48.8 0.7 copy-start.1
  49.1 0.7 copy-start.3
  49.8 6.6 %copy-start.4 = (s32[48,4]{0,1:T(4,128)S(1)}, s32[48,4]{0,1:T(4,128)}, u32[]{:S(2)}) copy-start(s32[48,4]{0,1:T(4,128)} %param.8) | copy-start | bytes 2308
  51.1 5.3 %copy-start.2 = (f32[4,48,4]{1,2,0:T(4,128)S(1)}, f32[4,48,4]{1,2,0:T(4,128)}, u32[]{:S(2)}) copy-start(f32[4,48,4]{1,2,0:T(4,128)} %param.9) | copy-start | bytes 9220
  51.1 6.9 %collective-permute-start = (f32[128,128]{1,0:T(8,128)S(1)}, f32[128,128]{1,0:T(8,128)S(1)}, u32[]{:S(2)}, u32[]{:S(2)}) collective-permute-start(f32[128,128]{1,0:T(8,128)S(1)} %get-tuple-element.9), channel_id=1, source_target_pairs={{0,64},{64,128},{128,192},{192,256},{256,320},{320,384},{384,448},... | collective-permute-start | bytes 196616 | tf_op jit(solution)/shard_map/ppermute | solution.py:148
  53.0 7.4 %collective-permute-start.1 = (f32[128,128]{1,0:T(8,128)S(1)}, f32[128,128]{1,0:T(8,128)S(1)}, u32[]{:S(2)}, u32[]{:S(2)}) collective-permute-start(f32[128,128]{1,0:T(8,128)S(1)} %get-tuple-element.10), channel_id=1, source_target_pairs={{64,0},{128,64},{192,128},{256,192},{320,256},{384,320},{448,384},... | collective-permute-start | bytes 196616 | tf_op jit(solution)/shard_map/ppermute | solution.py:149

commit v3 on v2

v3 whole, which is shorter than its diff:
```python
import functools

import jax
import jax.numpy as jnp
from jax import lax
from jax.experimental import pallas as pl
from jax.experimental.pallas import tpu as pltpu
from jax.sharding import PartitionSpec as P

TMAX = 6
REACH = 8
VMEM = pltpu.VMEM
SMEM = pltpu.SMEM
DMA = pltpu.SemaphoreType.DMA
PARAMS = pltpu.CompilerParams(vmem_limit_bytes=8 * 1024 * 1024)


def columns_first(x_ref, lo, o_ref, place):
    groups, per_block, _ = o_ref.shape
    o_ref[:, :, place : place + 128] = x_ref[lo : lo + 128, :].T.reshape(groups, per_block, 128)


def rows_first(x_ref, place):
    groups, per_block, _ = x_ref.shape
    return x_ref[:, :, place : place + 128].reshape(groups * per_block, 128).T


def split_kernel(x_ref, *refs):
    count = (len(refs) - 4) // 2
    o_ref = refs[count]
    in_ref, x_sem, t_sem = refs[-3:]
    blocks = x_ref.shape[0] // 128
    copies = []
    for i in range(blocks):
        block = pl.ds(i * 128, 128)
        copies.append(pltpu.make_async_copy(x_ref.at[block], in_ref.at[block], x_sem.at[i]))
        copies[-1].start()
    tables = []
    for i in range(count):
        tables.append(pltpu.make_async_copy(refs[i], refs[count + 1 + i], t_sem.at[i]))
        tables[-1].start()
    for i in range(blocks):
        copies[i].wait()
        columns_first(in_ref, i * 128, o_ref, i * 128)
    for copy in tables:
        copy.wait()


def last_kernel(x_ref, o_ref, out_ref, sem):
    copies = []
    for i in range(out_ref.shape[0] // 128):
        block = pl.ds(i * 128, 128)
        out_ref[i * 128 : (i + 1) * 128, :] = rows_first(x_ref, i * 128)
        copies.append(pltpu.make_async_copy(out_ref.at[block], o_ref.at[block], sem.at[i]))
        copies[-1].start()
    for copy in copies:
        copy.wait()


def rotate(line, offset, weights, ext_ref, cells, lanes_per_block):
    lanes = line.shape[1]
    circle = lanes // lanes_per_block * cells
    wrapped = offset & (circle - 1)
    rest = wrapped & (cells - 1)
    step = (wrapped >> (cells.bit_length() - 1)) * lanes_per_block
    before = (step + lanes_per_block) & (lanes - 1)
    after = (step + lanes - lanes_per_block) & (lanes - 1)
    ext_ref[0:cells] = pltpu.roll(line, before, 1)
    ext_ref[cells : 2 * cells] = pltpu.roll(line, step, 1)
    ext_ref[2 * cells : 2 * cells + 8] = pltpu.roll(line[0:8], after, 1)
    total = None
    for k in range(4):
        term = weights[k] * ext_ref[pl.ds(cells - 1 - rest + k, cells), :]
        total = term if total is None else total + term
    return total


def level_here(levels):
    return lax.div(lax.axis_index("lon") * levels, lax.axis_size("lon"))


def first_pass(x_ref, place, row, level, off_ref, w_ref, turn_ref, ext_ref, cells, outs):
    per_block = x_ref.shape[1]
    turn_ref[...] = rows_first(x_ref, place)
    for i in range(128 // cells):
        r = row + i
        value = rotate(
            turn_ref[i * cells : (i + 1) * cells, :],
            off_ref[level, r],
            [w_ref[k, level, r] for k in range(4)],
            ext_ref.at[r],
            cells,
            per_block,
        )
        for ref, start in outs:
            ref[start + i * cells : start + (i + 1) * cells, :] = value


def edge_kernel(cells, levels, rows, x_ref, off_ref, w_ref, head_ref, tail_ref, turn_ref, ext_ref):
    level = level_here(levels)
    for j, (row, ref) in enumerate(((0, head_ref), (rows - REACH, tail_ref))):
        first_pass(x_ref, row * cells, row, level, off_ref, w_ref, turn_ref.at[j], ext_ref, cells, [(ref, 0)])


def rows_done(chosen, rows, cells, levels, source_ref, first_place, scalars, o_ref, turn_ref, ext_ref):
    off_ref, w_ref, toff_ref, tw_ref = scalars
    level = level_here(levels)
    first_row = lax.axis_index("band") * rows
    last_row = lax.axis_size("band") * rows - 1
    for r in chosen:
        shift = toff_ref[level, r]
        total = None
        for k in range(4):
            source = jnp.clip(first_row + (r + k - 1) - shift, 0, last_row) - first_row - first_place
            term = tw_ref[k, level, r] * source_ref[pl.ds(pl.multiple_of(source * cells, cells), cells), :]
            total = term if total is None else total + term
        turn_ref[r * cells : (r + 1) * cells, :] = rotate(
            total, off_ref[level, r], [w_ref[k, level, r] for k in range(4)], ext_ref.at[r], cells, o_ref.shape[1]
        )
    per_turn = 128 // cells
    for i in sorted({r // per_turn for r in chosen}):
        columns_first(turn_ref, i * 128, o_ref, i * 128)


def inner_kernel(
    cells, levels, x_ref, head_ref, tail_ref, off_ref, w_ref, toff_ref, tw_ref, o_ref, near_ref, all_ref, turn_ref, ext_ref
):
    flat = o_ref.shape[2]
    rows = flat // cells
    edge = REACH * cells
    level = level_here(levels)
    all_ref[0:edge] = head_ref[...]
    all_ref[flat - edge : flat] = tail_ref[...]
    for place in range(edge, flat - edge, 128):
        outs = [(all_ref, place)]
        if place < 2 * edge:
            outs.append((near_ref, place - edge))
        if place >= flat - 2 * edge:
            outs.append((near_ref, place - (flat - 2 * edge) + edge))
        turn = turn_ref.at[place : place + 128]
        first_pass(x_ref, place, place // cells, level, off_ref, w_ref, turn, ext_ref, cells, outs)
    scalars = (off_ref, w_ref, toff_ref, tw_ref)
    rows_done(range(REACH, rows - REACH), rows, cells, levels, all_ref, 0, scalars, o_ref, turn_ref, ext_ref)


def outer_kernel(
    cells, levels, lo_ref, head_ref, near_ref, tail_ref, hi_ref, off_ref, w_ref, toff_ref, tw_ref, i_ref, o_ref, all_ref, turn_ref, ext_ref
):
    flat = o_ref.shape[2]
    rows = flat // cells
    edge = REACH * cells
    scalars = (off_ref, w_ref, toff_ref, tw_ref)
    all_ref[0:edge] = lo_ref[...]
    all_ref[edge : 2 * edge] = head_ref[...]
    all_ref[2 * edge : 3 * edge] = near_ref[0:edge]
    all_ref[flat - edge : flat] = near_ref[edge : 2 * edge]
    all_ref[flat : flat + edge] = tail_ref[...]
    all_ref[flat + edge : flat + 2 * edge] = hi_ref[...]
    chosen = [*range(REACH), *range(rows - REACH, rows)]
    rows_done(chosen, rows, cells, levels, all_ref, -REACH, scalars, o_ref, turn_ref, ext_ref)


def exchanged(x):
    return lax.all_to_all(x, "lon", 0, 0, tiled=True)


def per_device(tracers, lon_offset, lon_weights, lat_offset, lat_weights):
    rows, cells, columns = tracers.shape
    levels = lon_offset.shape[1]
    groups = lax.axis_size("lon")
    per_block = columns // groups
    bands = lax.axis_size("band")
    flat = rows * cells
    edge = REACH * cells
    f32 = jnp.float32
    vspec = pl.BlockSpec(memory_space=VMEM)
    sspec = pl.BlockSpec(memory_space=SMEM)
    scalars = (lon_offset.T, lon_weights.transpose(0, 2, 1), lat_offset.T, lat_weights.transpose(0, 2, 1))
    ext = VMEM((rows, 2 * cells + 8, columns), f32)

    def slabs(*lanes):
        return [jax.ShapeDtypeStruct((groups, per_block, n), f32) for n in lanes]

    def lines(*counts):
        return [jax.ShapeDtypeStruct((n, columns), f32) for n in counts]

    spread, *scalars = pl.pallas_call(
        split_kernel,
        out_shape=slabs(flat) + [jax.ShapeDtypeStruct(x.shape, x.dtype) for x in scalars],
        in_specs=[pl.BlockSpec(memory_space=pltpu.HBM)] * 5,
        out_specs=[vspec] * 5,
        scratch_shapes=[VMEM((flat, columns), f32), DMA((flat // 128,)), DMA((4,))],
        compiler_params=PARAMS,
        name="split",
    )(*(pltpu.with_memory_space_constraint(x, pltpu.HBM) for x in (tracers.reshape(flat, columns), *scalars)))
    gathered = exchanged(spread)
    head, tail = pl.pallas_call(
        functools.partial(edge_kernel, cells, levels, rows),
        out_shape=lines(edge, edge),
        in_specs=[vspec, sspec, sspec],
        out_specs=[vspec] * 2,
        scratch_shapes=[VMEM((2, 128, columns), f32), ext],
        compiler_params=PARAMS,
        name="edge",
    )(gathered, *scalars[:2])
    lo = lax.ppermute(tail, "band", [(i, i + 1) for i in range(bands - 1)])
    hi = lax.ppermute(head, "band", [(i + 1, i) for i in range(bands - 1)])
    inner, near = pl.pallas_call(
        functools.partial(inner_kernel, cells, levels),
        out_shape=slabs(flat) + lines(2 * edge),
        in_specs=[vspec] * 3 + [sspec] * 4,
        out_specs=[vspec] * 2,
        scratch_shapes=[VMEM((flat, columns), f32), VMEM((flat, columns), f32), ext],
        compiler_params=PARAMS,
        name="inner",
    )(gathered, head, tail, *scalars)
    (out,) = pl.pallas_call(
        functools.partial(outer_kernel, cells, levels),
        out_shape=slabs(flat),
        in_specs=[vspec] * 5 + [sspec] * 4 + [vspec],
        out_specs=[vspec],
        scratch_shapes=[VMEM((flat + 2 * edge, columns), f32), VMEM((flat, columns), f32), ext],
        input_output_aliases={9: 0},
        compiler_params=PARAMS,
        name="outer",
    )(lo, head, near, tail, hi, *scalars, inner)
    (last,) = pl.pallas_call(
        last_kernel,
        out_shape=lines(flat),
        in_specs=[vspec],
        out_specs=[pl.BlockSpec(memory_space=pltpu.HBM)],
        scratch_shapes=[VMEM((flat, columns), f32), DMA((flat // 128,))],
        compiler_params=PARAMS,
        name="last",
    )(exchanged(out))
    return last.reshape(rows, cells, columns)


def solution(mesh):
    return jax.shard_map(
        per_device,
        mesh=mesh,
        in_specs=(
            P("band", "lon", None),
            P("band", None),
            P(None, "band", None),
            P("band", None),
            P(None, "band", None),
        ),
        out_specs=P("band", "lon", None),
        check_vma=False,
    )
```

time: 98.2 us -> 96.6 us (0.984)
  local copies, waits for them, and re-layouts: 2.68 us -> 0 us
  Pallas kernels: 5.25 us -> 6.96 us
    pallas_call x5, Pallas kernels: 5.25 us -> 6.96 us  [the longest x1 2.12 us: per_device(): pl.pallas_call(functools.partial(inner_kernel, cells, levels), out_shape=...]
    unnamed x10 -> x0, local copies, waits for them, and re-layouts: 1.68 us -> none
    reshape x4 -> x0, local copies, waits for them, and re-layouts: 0.99 us -> none  [the longest x2 0.54 us: spread(): return y.reshape(n, m)]
where the time goes in v3:
time: 96.6 us; the launch traced here: 96.3 us
  blocking collectives  82.2 us (85%)
  Pallas kernels  6.96 us (7%)
  starting transfers between devices  5.28 us (5%)
  waiting for transfers between devices  1.89 us (2%)
    all_to_all x2, blocking collectives, exchanged(): return lax.all_to_all(x, 'lon', 0, 0, tiled=True)  82.2 us
    ppermute x1, starting transfers between devices, per_device(): hi = lax.ppermute(head, 'band', [(i + 1, i) for i in range(bands - 1)])  3.36 us
    pallas_call x1, Pallas kernels, per_device(): pl.pallas_call(functools.partial(inner_kernel, cells, levels), out_shape=...  2.12 us
  transfers between devices with their start and end apart: 2, of which 1 were waited for; matrix products, arithmetic and copies ran while one was open for 0% of the time, Pallas kernels for 2%

profile of v3, /device:TPU:25, one launch (start us, length us, event | category | flops | bytes accessed | tf_op | source)
XLA Modules:
  0.0 96.3 jit_solution(18269914154308723085)
XLA Ops:
  0.0 1.6 %split.1 = (f32[64,2,768]{2,1,0:T(2,128)S(1)}, s32[4,48]{1,0:T(4,128)S(1)}, f32[4,4,48]{2,1,0:T(4,128)S(1)}, s32[4,48]{1,0:T(4,128)S(1)}, f32[4,4,48]{2,1,0:T(4,128)S(1)}) custom-call(f32[768,128]{1,0:T(8,128)} %bitcast.6, s32[4,48]{1,0:T(4,128)} %bitcast.9, f32[4,4,48]{2,1,0:T(4,128)} %bitcast.7, s32[4,48]{1,0:T(4,128)} %bitcast.10, f32[4,4,48]{2,1,0:T(4,128)} %bitcast.8), custom_call_target="tpu_custom_call" | custom-call | tf_op jit(solution)/shard_map/split/pallas_call | solution.py:187
  1.6 47.4 %all_to_all.10.x_ref = f32[64,2,768]{2,1,0:T(2,128)S(1)} all-to-all(f32[64,2,768]{2,1,0:T(2,128)S(1)} %get-tuple-element.14), channel_id=1, replica_groups=mesh['band'=8,'lon'=64] {'lon'}, dimensions={0} | all-to-all | bytes 786432 | tf_op jit(solution)/shard_map/all_to_all | solution.py:164
  49.0 1.1 %edge.1 = (f32[128,128]{1,0:T(8,128)S(1)}, f32[128,128]{1,0:T(8,128)S(1)}) custom-call(f32[64,2,768]{2,1,0:T(2,128)S(1)} %all_to_all.10.x_ref, s32[4,48]{1,0:T(4,128)S(1)} %get-tuple-element.15.off_ref, f32[4,4,48]{2,1,0:T(4,128)S(1)} %get-tuple-element.16.w_ref), custom_call_target="tpu_custom_call" | custom-call | tf_op jit(solution)/shard_map/edge/pallas_call | solution.py:197
  50.1 1.9 %collective-permute-start = (f32[128,128]{1,0:T(8,128)S(1)}, f32[128,128]{1,0:T(8,128)S(1)}, u32[]{:S(2)}, u32[]{:S(2)}) collective-permute-start(f32[128,128]{1,0:T(8,128)S(1)} %get-tuple-element.17.tail_ref), channel_id=1, source_target_pairs={{0,64},{64,128},{128,192},{192,256},{256,320},{320,384},{384,448},... | collective-permute-start | bytes 196616 | tf_op jit(solution)/shard_map/ppermute | solution.py:206
  52.0 3.4 %collective-permute-start.1 = (f32[128,128]{1,0:T(8,128)S(1)}, f32[128,128]{1,0:T(8,128)S(1)}, u32[]{:S(2)}, u32[]{:S(2)}) collective-permute-start(f32[128,128]{1,0:T(8,128)S(1)} %get-tuple-element.18.head_ref), channel_id=1, source_target_pairs={{64,0},{128,64},{192,128},{256,192},{320,256},{384,320},{448,384},... | collective-permute-start | bytes 196616 | tf_op jit(solution)/shard_map/ppermute | solution.py:207
  55.4 2.1 %inner.1 = (f32[64,2,768]{2,1,0:T(2,128)S(1)}, f32[256,128]{1,0:T(8,128)S(1)}) custom-call(f32[64,2,768]{2,1,0:T(2,128)S(1)} %all_to_all.10.x_ref, f32[128,128]{1,0:T(8,128)S(1)} %get-tuple-element.18.head_ref, f32[128,128]{1,0:T(8,128)S(1)} %get-tuple-element.17.tail_ref, s32[4,48]{1,0:T(4,128)S(1)} %get-tuple-element.15.off_ref, ...), custom_call_target="tpu_custom_call" | custom-call | tf_op jit(solution)/shard_map/inner/pallas_call | solution.py:208
  57.5 0.0 collective-permute-done.lo_ref
  57.5 1.9 %collective-permute-done.1.hi_ref = f32[128,128]{1,0:T(8,128)S(1)} collective-permute-done((f32[128,128]{1,0:T(8,128)S(1)}, f32[128,128]{1,0:T(8,128)S(1)}, u32[]{:S(2)}, u32[]{:S(2)}) %collective-permute-start.1) | collective-permute-done | bytes 65568 | tf_op jit(solution)/shard_map/ppermute | solution.py:207
  59.4 1.3 %outer.1 = f32[64,2,768]{2,1,0:T(2,128)S(1)} custom-call(f32[128,128]{1,0:T(8,128)S(1)} %collective-permute-done.lo_ref, f32[128,128]{1,0:T(8,128)S(1)} %get-tuple-element.18.head_ref, f32[256,128]{1,0:T(8,128)S(1)} %get-tuple-element.21.near_ref, f32[128,128]{1,0:T(8,128)S(1)} %get-tuple-element.17.tail_ref, ...), custom_call_target="tpu_custom_call", output_to_operand_aliasing={{}: (9, {})} | custom-call | tf_op jit(solution)/shard_map/outer/pallas_call | solution.py:217
  60.7 34.8 %all_to_all.11.x_ref = f32[64,2,768]{2,1,0:T(2,128)S(1)} all-to-all(f32[64,2,768]{2,1,0:T(2,128)S(1)} %outer.1), channel_id=1, replica_groups=mesh['band'=8,'lon'=64] {'lon'}, dimensions={0} | all-to-all | bytes 786432 | tf_op jit(solution)/shard_map/all_to_all | solution.py:164
  95.5 0.9 last.1
Async XLA Ops:
  50.1 7.4 %collective-permute-start = (f32[128,128]{1,0:T(8,128)S(1)}, f32[128,128]{1,0:T(8,128)S(1)}, u32[]{:S(2)}, u32[]{:S(2)}) collective-permute-start(f32[128,128]{1,0:T(8,128)S(1)} %get-tuple-element.17.tail_ref), channel_id=1, source_target_pairs={{0,64},{64,128},{128,192},{192,256},{256,320},{320,384},{384,448},... | collective-permute-start | bytes 196616 | tf_op jit(solution)/shard_map/ppermute | solution.py:206
  52.0 7.4 %collective-permute-start.1 = (f32[128,128]{1,0:T(8,128)S(1)}, f32[128,128]{1,0:T(8,128)S(1)}, u32[]{:S(2)}, u32[]{:S(2)}) collective-permute-start(f32[128,128]{1,0:T(8,128)S(1)} %get-tuple-element.18.head_ref), channel_id=1, source_target_pairs={{64,0},{128,64},{192,128},{256,192},{320,256},{384,320},{448,384},... | collective-permute-start | bytes 196616 | tf_op jit(solution)/shard_map/ppermute | solution.py:207

commit v4 on v3

--- a/solution.py
+++ b/solution.py
@@ -186,13 +186,14 @@
 
     spread, *scalars = pl.pallas_call(
         split_kernel,
-        out_shape=slabs(flat) + [jax.ShapeDtypeStruct(x.shape, x.dtype) for x in scalars],
+        out_shape=slabs(flat) + [SMEM(x.shape, x.dtype) for x in scalars],
         in_specs=[pl.BlockSpec(memory_space=pltpu.HBM)] * 5,
-        out_specs=[vspec] * 5,
+        out_specs=[vspec] + [sspec] * 4,
         scratch_shapes=[VMEM((flat, columns), f32), DMA((flat // 128,)), DMA((4,))],
         compiler_params=PARAMS,
         name="split",
     )(*(pltpu.with_memory_space_constraint(x, pltpu.HBM) for x in (tracers.reshape(flat, columns), *scalars)))
+    scalars = [pltpu.with_memory_space_constraint(x, SMEM) for x in scalars]
     gathered = exchanged(spread)
     head, tail = pl.pallas_call(
         functools.partial(edge_kernel, cells, levels, rows),

time: 96.6 us -> 95.1 us (0.984)
  Pallas kernels: 6.96 us -> 4.6 us
  transfers between devices with their start and end apart: 2 -> 2, of which waited for: 1 -> 1; matrix products, arithmetic and copies ran while one was open for 0% -> 0% of each run, Pallas kernels for 2% -> 1%
where the time goes in v4:
time: 95.1 us; the launch traced here: 94.8 us
  blocking collectives  82.2 us (86%)
  starting transfers between devices  5.28 us (6%)
  Pallas kernels  4.6 us (5%)
  waiting for transfers between devices  2.72 us (3%)
    all_to_all x2, blocking collectives, exchanged(): return lax.all_to_all(x, 'lon', 0, 0, tiled=True)  82.2 us
    ppermute x1, starting transfers between devices, per_device(): hi = lax.ppermute(head, 'band', [(i + 1, i) for i in range(bands - 1)])  3.36 us
    ppermute x1, waiting for transfers between devices, per_device(): hi = lax.ppermute(head, 'band', [(i + 1, i) for i in range(bands - 1)])  2.72 us
    ppermute x1, starting transfers between devices, per_device(): lo = lax.ppermute(tail, 'band', [(i, i + 1) for i in range(bands - 1)])  1.92 us
  transfers between devices with their start and end apart: 2, of which 1 were waited for; matrix products, arithmetic and copies ran while one was open for 0% of the time, Pallas kernels for 1%

profile of v4, /device:TPU:25, one launch (start us, length us, event | category | flops | bytes accessed | tf_op | source)
XLA Modules:
  0.0 94.8 jit_solution(5870660517520851505)
XLA Ops:
  0.0 1.6 %split.1 = (f32[64,2,768]{2,1,0:T(2,128)S(1)}, s32[4,48]{1,0:T(4,128)S(4)}, f32[4,4,48]{2,1,0:T(4,128)S(4)}, s32[4,48]{1,0:T(4,128)S(4)}, f32[4,4,48]{2,1,0:T(4,128)S(4)}) custom-call(f32[768,128]{1,0:T(8,128)} %bitcast.6, s32[4,48]{1,0:T(4,128)} %bitcast.9, f32[4,4,48]{2,1,0:T(4,128)} %bitcast.7, s32[4,48]{1,0:T(4,128)} %bitcast.10, f32[4,4,48]{2,1,0:T(4,128)} %bitcast.8), custom_call_target="tpu_custom_call" | custom-call | tf_op jit(solution)/shard_map/split/pallas_call | solution.py:187
  1.6 47.4 %all_to_all.10.x_ref = f32[64,2,768]{2,1,0:T(2,128)S(1)} all-to-all(f32[64,2,768]{2,1,0:T(2,128)S(1)} %get-tuple-element.14), channel_id=1, replica_groups=mesh['band'=8,'lon'=64] {'lon'}, dimensions={0} | all-to-all | bytes 786432 | tf_op jit(solution)/shard_map/all_to_all | solution.py:164
  49.0 0.4 edge.1
  49.4 1.9 %collective-permute-start = (f32[128,128]{1,0:T(8,128)S(1)}, f32[128,128]{1,0:T(8,128)S(1)}, u32[]{:S(2)}, u32[]{:S(2)}) collective-permute-start(f32[128,128]{1,0:T(8,128)S(1)} %get-tuple-element.17.tail_ref), channel_id=1, source_target_pairs={{0,64},{64,128},{128,192},{192,256},{256,320},{320,384},{384,448},... | collective-permute-start | bytes 196616 | tf_op jit(solution)/shard_map/ppermute | solution.py:207
  51.3 3.4 %collective-permute-start.1 = (f32[128,128]{1,0:T(8,128)S(1)}, f32[128,128]{1,0:T(8,128)S(1)}, u32[]{:S(2)}, u32[]{:S(2)}) collective-permute-start(f32[128,128]{1,0:T(8,128)S(1)} %get-tuple-element.18.head_ref), channel_id=1, source_target_pairs={{64,0},{128,64},{192,128},{256,192},{320,256},{384,320},{448,384},... | collective-permute-start | bytes 196616 | tf_op jit(solution)/shard_map/ppermute | solution.py:208
  54.7 1.3 %inner.1 = (f32[64,2,768]{2,1,0:T(2,128)S(1)}, f32[256,128]{1,0:T(8,128)S(1)}) custom-call(f32[64,2,768]{2,1,0:T(2,128)S(1)} %all_to_all.10.x_ref, f32[128,128]{1,0:T(8,128)S(1)} %get-tuple-element.18.head_ref, f32[128,128]{1,0:T(8,128)S(1)} %get-tuple-element.17.tail_ref, s32[4,48]{1,0:T(4,128)S(4)} %get-tuple-element.15.off_ref, ...), custom_call_target="tpu_custom_call" | custom-call | tf_op jit(solution)/shard_map/inner/pallas_call | solution.py:209
  56.0 0.0 collective-permute-done.lo_ref
  56.0 2.7 %collective-permute-done.1.hi_ref = f32[128,128]{1,0:T(8,128)S(1)} collective-permute-done((f32[128,128]{1,0:T(8,128)S(1)}, f32[128,128]{1,0:T(8,128)S(1)}, u32[]{:S(2)}, u32[]{:S(2)}) %collective-permute-start.1) | collective-permute-done | bytes 65568 | tf_op jit(solution)/shard_map/ppermute | solution.py:208
  58.7 0.4 outer.1
  59.1 34.8 %all_to_all.11.x_ref = f32[64,2,768]{2,1,0:T(2,128)S(1)} all-to-all(f32[64,2,768]{2,1,0:T(2,128)S(1)} %outer.1), channel_id=1, replica_groups=mesh['band'=8,'lon'=64] {'lon'}, dimensions={0} | all-to-all | bytes 786432 | tf_op jit(solution)/shard_map/all_to_all | solution.py:164
  93.9 0.9 last.1
Async XLA Ops:
  49.4 6.6 %collective-permute-start = (f32[128,128]{1,0:T(8,128)S(1)}, f32[128,128]{1,0:T(8,128)S(1)}, u32[]{:S(2)}, u32[]{:S(2)}) collective-permute-start(f32[128,128]{1,0:T(8,128)S(1)} %get-tuple-element.17.tail_ref), channel_id=1, source_target_pairs={{0,64},{64,128},{128,192},{192,256},{256,320},{320,384},{384,448},... | collective-permute-start | bytes 196616 | tf_op jit(solution)/shard_map/ppermute | solution.py:207
  51.3 7.4 %collective-permute-start.1 = (f32[128,128]{1,0:T(8,128)S(1)}, f32[128,128]{1,0:T(8,128)S(1)}, u32[]{:S(2)}, u32[]{:S(2)}) collective-permute-start(f32[128,128]{1,0:T(8,128)S(1)} %get-tuple-element.18.head_ref), channel_id=1, source_target_pairs={{64,0},{128,64},{192,128},{256,192},{320,256},{384,320},{448,384},... | collective-permute-start | bytes 196616 | tf_op jit(solution)/shard_map/ppermute | solution.py:208

commit v5 on v0

v5 whole, which is shorter than its diff:
```python
import functools

import jax
import jax.numpy as jnp
from jax import lax
from jax.experimental import pallas as pl
from jax.experimental.pallas import tpu as pltpu
from jax.sharding import PartitionSpec as P


REACH = 8
PARTS = 2
VMEM = pltpu.VMEM
SMEM = pltpu.SMEM
DMA = pltpu.SemaphoreType.DMA
PARAMS = pltpu.CompilerParams(vmem_limit_bytes=8 * 1024 * 1024)


def columns_first(block, groups):
    return block.T.reshape(groups, block.shape[1] // groups, block.shape[0])


def rows_first(slab):
    return slab.reshape(slab.shape[0] * slab.shape[1], slab.shape[2]).T


def split_kernel(x_ref, *refs):
    count = (len(refs) - 4) // 2
    o_ref = refs[count]
    in_ref, x_sem, t_sem = refs[-3:]
    pairs, cores, slabs, sets, per_set, _ = o_ref.shape
    part = x_ref.shape[0] // PARTS
    copies = []
    for i in range(PARTS):
        block = pl.ds(i * part, part)
        copies.append(pltpu.make_async_copy(x_ref.at[block], in_ref.at[block], x_sem.at[i]))
        copies[-1].start()
    tables = []
    for i in range(count):
        tables.append(pltpu.make_async_copy(refs[i], refs[count + 1 + i], t_sem.at[i]))
        tables[-1].start()
    for i in range(cores * slabs):
        if i * 128 % part == 0:
            copies[i * 128 // part].wait()
        value = columns_first(in_ref[i * 128 : (i + 1) * 128, :], pairs * sets).reshape(pairs, sets, per_set, 128)
        o_ref[:, i // slabs, i % slabs] = value
    for copy in tables:
        copy.wait()


def last_kernel(x_ref, o_ref, out_ref, sem):
    pairs, cores, slabs, sets, per_set, _ = x_ref.shape
    copies = []
    for i in range(cores * slabs):
        block = pl.ds(i * 128, 128)
        value = x_ref[:, i // slabs, i % slabs].reshape(pairs * sets, per_set, 128)
        out_ref[i * 128 : (i + 1) * 128, :] = rows_first(value)
        copies.append(pltpu.make_async_copy(out_ref.at[block], o_ref.at[block], sem.at[i]))
        copies[-1].start()
    for copy in copies:
        copy.wait()


def rotate(lines, offset, weights, ext_refs, cells, lanes_per_block):
    lanes = lines[0].shape[1]
    circle = lanes // lanes_per_block * cells
    wrapped = offset & (circle - 1)
    rest = wrapped & (cells - 1)
    step = (wrapped >> (cells.bit_length() - 1)) * lanes_per_block
    before = (step + lanes_per_block) & (lanes - 1)
    after = (step + lanes - lanes_per_block) & (lanes - 1)
    totals = []
    for line, ext_ref in zip(lines, ext_refs):
        ext_ref[0:cells] = pltpu.roll(line, before, 1)
        ext_ref[cells : 2 * cells] = pltpu.roll(line, step, 1)
        ext_ref[2 * cells : 2 * cells + 8] = pltpu.roll(line[0:8], after, 1)
        total = None
        for k in range(4):
            term = weights[k] * ext_ref[pl.ds(cells - 1 - rest + k, cells), :]
            total = term if total is None else total + term
        totals.append(total)
    return totals


def here(levels):
    lon = lax.axis_index("lon")
    return lax.div(lon * levels, lax.axis_size("lon")), lax.rem(lon, 2)


def first_pass(x_ref, slab, row, level, off_ref, w_ref, o_ref, turn_ref, ext_ref, cells):
    sets, per_set = x_ref.shape[2:4]
    for g in range(sets):
        turn_ref[g] = rows_first(x_ref[:, slab, g])
    for i in range(128 // cells):
        place = slice(i * cells, (i + 1) * cells)
        values = rotate(
            [turn_ref[g, place, :] for g in range(sets)],
            off_ref[level, row + i],
            [w_ref[k, level, row + i] for k in range(4)],
            [ext_ref.at[i, g] for g in range(sets)],
            cells,
            per_set,
        )
        for g in range(sets):
            o_ref[g * 128 + i * cells : g * 128 + (i + 1) * cells, :] = values[g]


def rows_done(slab, half, window_ref, first_place, level, core, tables, o_ref, turn_ref, ext_ref, cells):
    off_ref, w_ref, toff_ref, tw_ref = tables
    groups, _, sets, per_set, _ = o_ref.shape
    rows = 2 * half
    per_slab = 128 // cells
    first_row = lax.axis_index("band") * rows
    last_row = lax.axis_size("band") * rows - 1
    half_row = core * half
    for i in range(per_slab):
        row = half_row + slab * per_slab + i
        shift = toff_ref[level, row]
        totals = [None] * sets
        for k in range(4):
            source = jnp.clip(first_row + row + (k - 1) - shift, 0, last_row) - first_row - half_row - first_place
            weight = tw_ref[k, level, row]
            where = pl.ds(pl.multiple_of(source * cells, cells), cells)
            for g in range(sets):
                term = weight * window_ref[g, where, :]
                totals[g] = term if totals[g] is None else totals[g] + term
        values = rotate(
            totals,
            off_ref[level, row],
            [w_ref[k, level, row] for k in range(4)],
            [ext_ref.at[per_slab + i, g] for g in range(sets)],
            cells,
            per_set,
        )
        for g in range(sets):
            turn_ref[g, i * cells : (i + 1) * cells, :] = values[g]
    for g in range(sets):
        o_ref[:, slab, g] = columns_first(turn_ref[g], groups)


def edge_kernel(cells, levels, half, far, x_ref, off_ref, w_ref, o_ref, turn_ref, ext_ref):
    level, core = here(levels)
    slab = (core if far else 1 - core) * (x_ref.shape[1] - 1)
    row = core * half + slab * (128 // cells)
    first_pass(x_ref, slab, row, level, off_ref, w_ref, o_ref, turn_ref, ext_ref, cells)


def inner_kernel(
    cells, levels, half, x_ref, far_ref, near_ref, off_ref, w_ref, toff_ref, tw_ref, o_ref, mid_ref, own_ref, turn_ref, ext_ref
):
    level, core = here(levels)
    sets = x_ref.shape[2]
    row = core * half + 128 // cells
    first_pass(x_ref, 1, row, level, off_ref, w_ref, mid_ref, turn_ref, ext_ref, cells)
    for g in range(sets):
        part = slice(g * 128, (g + 1) * 128)
        own_ref[g, pl.ds(pl.multiple_of(core * 256, 128), 128), :] = far_ref[part, :]
        own_ref[g, 128:256, :] = mid_ref[part, :]
        own_ref[g, pl.ds(pl.multiple_of((1 - core) * 256, 128), 128), :] = near_ref[part, :]
    tables = (off_ref, w_ref, toff_ref, tw_ref)
    rows_done(1, half, own_ref, 0, level, core, tables, o_ref, turn_ref, ext_ref, cells)


def side_kernel(
    cells, levels, half, far, edge_ref, mid_ref, halo_ref, off_ref, w_ref, toff_ref, tw_ref, i_ref, o_ref, own_ref, turn_ref, ext_ref
):
    level, core = here(levels)
    above = 1 - core if far else core
    sets = o_ref.shape[2]
    for g in range(sets):
        part = slice(g * 128, (g + 1) * 128)
        own_ref[g, pl.ds(pl.multiple_of((1 - above) * 256, 128), 128), :] = halo_ref[part, :]
        own_ref[g, 128:256, :] = edge_ref[part, :]
        own_ref[g, pl.ds(pl.multiple_of(above * 256, 128), 128), :] = mid_ref[part, :]
    slab = (1 - above) * 2
    first_place = (slab - 1) * (128 // cells)
    tables = (off_ref, w_ref, toff_ref, tw_ref)
    rows_done(slab, half, own_ref, first_place, level, core, tables, o_ref, turn_ref, ext_ref, cells)


def exchanged(x):
    return lax.all_to_all(x, "lon", 0, 0, tiled=True)


def per_device(tracers, lon_offset, lon_weights, lat_offset, lat_weights):
    rows, cells, columns = tracers.shape
    levels = lon_offset.shape[1]
    groups = lax.axis_size("lon")
    bands = lax.axis_size("band")
    flat = rows * cells
    half = rows // 2
    slabs = half * cells // 128
    per_set = 128 // groups
    sets = columns * 2 // groups // per_set
    f32 = jnp.float32
    vspec = pl.BlockSpec(memory_space=VMEM)
    sspec = pl.BlockSpec(memory_space=SMEM)
    hspec = pl.BlockSpec(memory_space=pltpu.HBM)
    tables = (lon_offset.T, lon_weights.transpose(0, 2, 1), lat_offset.T, lat_weights.transpose(0, 2, 1))
    assert slabs == 3 and REACH * cells == 128 and columns == 128
    sent = jax.ShapeDtypeStruct((groups // 2, 2, slabs, sets, per_set, 128), f32)
    slab_lines = jax.ShapeDtypeStruct((sets * 128, 128), f32)
    gathered_shape = (groups, *sent.shape[2:])
    turn = VMEM((sets, 128, 128), f32)
    ext = VMEM((2 * 128 // cells, sets, 2 * cells + 8, 128), f32)
    own = VMEM((sets, 3 * 128, 128), f32)

    def call(kernel, out_shape, in_specs, scratch, *args, aliases={}):
        return pl.pallas_call(
            kernel,
            out_shape=out_shape,
            in_specs=in_specs,
            out_specs=jax.tree.map(lambda x: vspec if isinstance(x, jax.ShapeDtypeStruct) else sspec, out_shape),
            scratch_shapes=scratch,
            input_output_aliases=aliases,
            compiler_params=PARAMS,
        )(*args)

    given = [pltpu.with_memory_space_constraint(x, pltpu.HBM) for x in (tracers.reshape(flat, columns), *tables)]
    spread, *tables = call(
        split_kernel,
        [sent] + [SMEM(x.shape, x.dtype) for x in tables],
        [hspec] * 5,
        [VMEM((flat, columns), f32), DMA((PARTS,)), DMA((4,))],
        *given,
    )
    tables = [pltpu.with_memory_space_constraint(x, SMEM) for x in tables]
    gathered = exchanged(spread.reshape(gathered_shape))

    def edge(far):
        kernel = functools.partial(edge_kernel, cells, levels, half, far)
        return call(kernel, slab_lines, [vspec, sspec, sspec], [turn, ext], gathered, *tables[:2])

    far = edge(True)
    pairs = []
    for n in range(bands - 1):
        for lon in range(1, groups, 2):
            lower, upper = n * groups + lon, (n + 1) * groups + lon - 1
            pairs += [(lower, upper), (upper, lower)]
    far_halo = lax.ppermute(far, ("band", "lon"), pairs)
    near = edge(False)
    near_halo = lax.ppermute(near, "lon", [(lon, lon ^ 1) for lon in range(groups)])
    out, mid = call(
        functools.partial(inner_kernel, cells, levels, half),
        [jax.ShapeDtypeStruct(gathered_shape, f32), slab_lines],
        [vspec] * 3 + [sspec] * 4,
        [own, turn, ext],
        gathered,
        far,
        near,
        *tables,
    )
    for is_far, edge_rows, halo in ((False, near, near_halo), (True, far, far_halo)):
        out = call(
            functools.partial(side_kernel, cells, levels, half, is_far),
            jax.ShapeDtypeStruct(gathered_shape, f32),
            [vspec] * 3 + [sspec] * 4 + [vspec],
            [own, turn, ext],
            edge_rows,
            mid,
            halo,
            *tables,
            out,
            aliases={7: 0},
        )
    last = pl.pallas_call(
        last_kernel,
        out_shape=jax.ShapeDtypeStruct((flat, columns), f32),
        in_specs=[vspec],
        out_specs=hspec,
        scratch_shapes=[VMEM((flat, columns), f32), DMA((flat // 128,))],
        compiler_params=PARAMS,
        name="last",
    )(exchanged(out).reshape(sent.shape))
    return last.reshape(rows, cells, columns)


def solution(mesh):
    return jax.shard_map(
        per_device,
        mesh=mesh,
        in_specs=(
            P("band", "lon", None),
            P("band", None),
            P(None, "band", None),
            P("band", None),
            P(None, "band", None),
        ),
        out_specs=P("band", "lon", None),
        check_vma=False,
    )
```

time: 378 us -> 94.4 us (0.25)
  the two profiles are of different devices: /device:TPU:8 before, /device:TPU:25 now
where the time goes in v5:
time: 94.4 us; the launch traced here: 94.2 us
  blocking collectives  80.7 us (85%)
  waiting for transfers between devices  5.11 us (5%)
  starting transfers between devices  4.18 us (4%)
  Pallas kernels  4.12 us (4%)
    all_to_all x2, blocking collectives, exchanged(): return lax.all_to_all(x, 'lon', 0, 0, tiled=True)  80.7 us
    ppermute x1, waiting for transfers between devices, per_device(): far_halo = lax.ppermute(far, ('band', 'lon'), pairs)  5.1 us
    pallas_call x6, Pallas kernels, call(): pl.pallas_call(kernel, out_shape=out_shape, in_specs=in_specs, out_specs=...  3.22 us
    ppermute x1, starting transfers between devices, per_device(): far_halo = lax.ppermute(far, ('band', 'lon'), pairs)  2.26 us
    ppermute x1, starting transfers between devices, per_device(): lax.ppermute(near, 'lon', [(lon, lon ^ 1) for lon in range(groups)])  1.92 us
  transfers between devices with their start and end apart: 2, of which 1 were waited for; matrix products, arithmetic and copies ran while one was open for 0% of the time, Pallas kernels for 1%

profile of v5, /device:TPU:25, one launch (start us, length us, event | category | flops | bytes accessed | tf_op | source)
XLA Modules:
  0.0 94.2 jit_solution(4353616922276026598)
XLA Ops:
  0.0 1.3 %shard_map.55 = (f32[32,2,3,2,2,128]{5,4,3,2,1,0:T(2,128)S(1)}, s32[4,48]{1,0:T(4,128)S(4)}, f32[4,4,48]{2,1,0:T(4,128)S(4)}, s32[4,48]{1,0:T(4,128)S(4)}, f32[4,4,48]{2,1,0:T(4,128)S(4)}) custom-call(f32[768,128]{1,0:T(8,128)} %bitcast.10, s32[4,48]{1,0:T(4,128)} %bitcast.13, f32[4,4,48]{2,1,0:T(4,128)} %bitcast.11, s32[4,48]{1,0:T(4,128)} %bitcast.14, ...), custom_call_target="tpu_custom_call" | custom-call | tf_op jit(solution)/shard_map/pallas_call | solution.py:209
  1.3 47.4 %all_to_all.10.x_ref = f32[64,3,2,2,128]{4,3,2,1,0:T(2,128)S(1)} all-to-all(f32[64,3,2,2,128]{4,3,2,1,0:T(2,128)S(1)} %bitcast.9), channel_id=1, replica_groups=mesh['band'=8,'lon'=64] {'lon'}, dimensions={0} | all-to-all | bytes 786432 | tf_op jit(solution)/shard_map/all_to_all | solution.py:182
  48.7 0.3 shard_map.57.near_ref.edge_ref
  49.0 1.9 %collective-permute-start.1 = (f32[256,128]{1,0:T(8,128)S(1)}, f32[256,128]{1,0:T(8,128)S(1)}, u32[]{:S(2)}, u32[]{:S(2)}) collective-permute-start(f32[256,128]{1,0:T(8,128)S(1)} %shard_map.57.near_ref.edge_ref), channel_id=1, source_target_pairs={{0,1},{1,0},{2,3},{3,2},{4,5},{5,4},{6,7},{7,6},{8,9},{9,8},{10,11... | collective-permute-start | bytes 393224 | tf_op jit(solution)/shard_map/ppermute | solution.py:242
  50.9 0.3 shard_map.56.far_ref.edge_ref
  51.2 2.3 %collective-permute-start = (f32[256,128]{1,0:T(8,128)S(1)}, f32[256,128]{1,0:T(8,128)S(1)}, u32[]{:S(2)}, u32[]{:S(2)}) collective-permute-start(f32[256,128]{1,0:T(8,128)S(1)} %shard_map.56.far_ref.edge_ref), channel_id=1, source_target_pairs={{1,64},{64,1},{3,66},{66,3},{5,68},{68,5},{7,70},{70,7},{9,72},{72... | collective-permute-start | bytes 393224 | tf_op jit(solution)/shard_map/ppermute | solution.py:240
  53.5 0.6 shard_map.58
  54.1 0.0 collective-permute-done.1.halo_ref
  54.1 0.4 shard_map.59.i_ref
  54.5 5.1 %collective-permute-done.halo_ref = f32[256,128]{1,0:T(8,128)S(1)} collective-permute-done((f32[256,128]{1,0:T(8,128)S(1)}, f32[256,128]{1,0:T(8,128)S(1)}, u32[]{:S(2)}, u32[]{:S(2)}) %collective-permute-start) | collective-permute-done | bytes 131104 | tf_op jit(solution)/shard_map/ppermute | solution.py:240
  59.6 0.4 shard_map.60
  60.0 33.3 %all_to_all.11 = f32[64,3,2,2,128]{4,3,2,1,0:T(2,128)S(1)} all-to-all(f32[64,3,2,2,128]{4,3,2,1,0:T(2,128)S(1)} %shard_map.60), channel_id=1, replica_groups=mesh['band'=8,'lon'=64] {'lon'}, dimensions={0} | all-to-all | bytes 786432 | tf_op jit(solution)/shard_map/all_to_all | solution.py:182
  93.3 0.9 last.1
Async XLA Ops:
  49.0 5.1 %collective-permute-start.1 = (f32[256,128]{1,0:T(8,128)S(1)}, f32[256,128]{1,0:T(8,128)S(1)}, u32[]{:S(2)}, u32[]{:S(2)}) collective-permute-start(f32[256,128]{1,0:T(8,128)S(1)} %shard_map.57.near_ref.edge_ref), channel_id=1, source_target_pairs={{0,1},{1,0},{2,3},{3,2},{4,5},{5,4},{6,7},{7,6},{8,9},{9,8},{10,11... | collective-permute-start | bytes 393224 | tf_op jit(solution)/shard_map/ppermute | solution.py:242
  51.2 8.4 %collective-permute-start = (f32[256,128]{1,0:T(8,128)S(1)}, f32[256,128]{1,0:T(8,128)S(1)}, u32[]{:S(2)}, u32[]{:S(2)}) collective-permute-start(f32[256,128]{1,0:T(8,128)S(1)} %shard_map.56.far_ref.edge_ref), channel_id=1, source_target_pairs={{1,64},{64,1},{3,66},{66,3},{5,68},{68,5},{7,70},{70,7},{9,72},{72... | collective-permute-start | bytes 393224 | tf_op jit(solution)/shard_map/ppermute | solution.py:240

commit v6 on v5

--- a/solution.py
+++ b/solution.py
@@ -169,7 +169,8 @@
     sets = o_ref.shape[2]
     for g in range(sets):
         part = slice(g * 128, (g + 1) * 128)
-        own_ref[g, pl.ds(pl.multiple_of((1 - above) * 256, 128), 128), :] = halo_ref[part, :]
+        halo = halo_ref[part, :] if far else halo_ref[1 - core, part, :]
+        own_ref[g, pl.ds(pl.multiple_of((1 - above) * 256, 128), 128), :] = halo
         own_ref[g, 128:256, :] = edge_ref[part, :]
         own_ref[g, pl.ds(pl.multiple_of(above * 256, 128), 128), :] = mid_ref[part, :]
     slab = (1 - above) * 2
@@ -239,7 +240,7 @@
             pairs += [(lower, upper), (upper, lower)]
     far_halo = lax.ppermute(far, ("band", "lon"), pairs)
     near = edge(False)
-    near_halo = lax.ppermute(near, "lon", [(lon, lon ^ 1) for lon in range(groups)])
+    near_halo = lax.all_gather(near, "lon", axis_index_groups=[[lon, lon + 1] for lon in range(0, groups, 2)])
     out, mid = call(
         functools.partial(inner_kernel, cells, levels, half),
         [jax.ShapeDtypeStruct(gathered_shape, f32), slab_lines],

time: 94.4 us -> 91.7 us (0.971)
  waiting for transfers between devices: 5.11 us -> 2.71 us
  starting transfers between devices: 4.18 us -> 1.92 us
  blocking collectives: 80.7 us -> 82.7 us
    all_gather x0 -> x1, blocking collectives: none -> 2.47 us  [per_device(): lax.all_gather(near, 'lon', axis_index_groups=[[lon, lon + 1] for lon in...]
    ppermute x1, waiting for transfers between devices: 5.1 us -> 2.71 us  [per_device(): far_halo = lax.ppermute(far, ('band', 'lon'), pairs)]
    ppermute x1 -> x0, starting transfers between devices: 1.92 us -> none  [per_device(): lax.ppermute(near, 'lon', [(lon, lon ^ 1) for lon in range(groups)])]
  transfers between devices with their start and end apart: 2 -> 1, of which waited for: 1 -> 1; matrix products, arithmetic and copies ran while one was open for 0% -> 0% of each run, Pallas kernels for 1% -> 1%
where the time goes in v6:
time: 91.7 us; the launch traced here: 91.5 us
  blocking collectives  82.7 us (90%)
  Pallas kernels  4.11 us (4%)
  waiting for transfers between devices  2.71 us (3%)
  starting transfers between devices  1.92 us (2%)
    all_to_all x2, blocking collectives, exchanged(): return lax.all_to_all(x, 'lon', 0, 0, tiled=True)  80.2 us
    pallas_call x6, Pallas kernels, call(): pl.pallas_call(kernel, out_shape=out_shape, in_specs=in_specs, out_specs=...  3.21 us
    ppermute x1, waiting for transfers between devices, per_device(): far_halo = lax.ppermute(far, ('band', 'lon'), pairs)  2.71 us
    all_gather x1, blocking collectives, per_device(): lax.all_gather(near, 'lon', axis_index_groups=[[lon, lon + 1] for lon in...  2.47 us
    ppermute x1, starting transfers between devices, per_device(): far_halo = lax.ppermute(far, ('band', 'lon'), pairs)  1.92 us
  transfers between devices with their start and end apart: 1, of which 1 were waited for; matrix products, arithmetic and copies ran while one was open for 0% of the time, Pallas kernels for 1%

profile of v6, /device:TPU:25, one launch (start us, length us, event | category | flops | bytes accessed | tf_op | source)
XLA Modules:
  0.0 91.5 jit_solution(7859489152428516027)
XLA Ops:
  0.0 1.3 %shard_map.55 = (f32[32,2,3,2,2,128]{5,4,3,2,1,0:T(2,128)S(1)}, s32[4,48]{1,0:T(4,128)S(4)}, f32[4,4,48]{2,1,0:T(4,128)S(4)}, s32[4,48]{1,0:T(4,128)S(4)}, f32[4,4,48]{2,1,0:T(4,128)S(4)}) custom-call(f32[768,128]{1,0:T(8,128)} %bitcast.12, s32[4,48]{1,0:T(4,128)} %bitcast.15, f32[4,4,48]{2,1,0:T(4,128)} %bitcast.13, s32[4,48]{1,0:T(4,128)} %bitcast.16, ...), custom_call_target="tpu_custom_call" | custom-call | tf_op jit(solution)/shard_map/pallas_call | solution.py:210
  1.3 47.4 %all_to_all.10.x_ref = f32[64,3,2,2,128]{4,3,2,1,0:T(2,128)S(1)} all-to-all(f32[64,3,2,2,128]{4,3,2,1,0:T(2,128)S(1)} %bitcast.11), channel_id=1, replica_groups=mesh['band'=8,'lon'=64] {'lon'}, dimensions={0} | all-to-all | bytes 786432 | tf_op jit(solution)/shard_map/all_to_all | solution.py:183
  48.7 0.3 shard_map.56.far_ref.edge_ref
  49.0 1.9 %collective-permute-start = (f32[256,128]{1,0:T(8,128)S(1)}, f32[256,128]{1,0:T(8,128)S(1)}, u32[]{:S(2)}, u32[]{:S(2)}) collective-permute-start(f32[256,128]{1,0:T(8,128)S(1)} %shard_map.56.far_ref.edge_ref), channel_id=1, source_target_pairs={{1,64},{64,1},{3,66},{66,3},{5,68},{68,5},{7,70},{70,7},{9,72},{72... | collective-permute-start | bytes 393224 | tf_op jit(solution)/shard_map/ppermute | solution.py:241
  50.9 0.3 shard_map.57.near_ref.edge_ref
  51.2 0.6 shard_map.58
  51.8 2.5 %all-gather = f32[512,128]{1,0:T(8,128)S(1)} all-gather(f32[256,128]{1,0:T(8,128)S(1)} %shard_map.57.near_ref.edge_ref), channel_id=2, replica_groups={{0,1},{2,3},{4,5},{6,7},{8,9},{10,11},{12,13},{14,15},{16,17},{18,19},{..., dimensions={0}, use_global_device_ids=true | all-gather | bytes 393216 | tf_op jit(solution)/shard_map/all_gather | solution.py:243
  54.3 0.4 shard_map.59.i_ref
  54.7 2.7 %collective-permute-done.halo_ref = f32[256,128]{1,0:T(8,128)S(1)} collective-permute-done((f32[256,128]{1,0:T(8,128)S(1)}, f32[256,128]{1,0:T(8,128)S(1)}, u32[]{:S(2)}, u32[]{:S(2)}) %collective-permute-start) | collective-permute-done | bytes 131104 | tf_op jit(solution)/shard_map/ppermute | solution.py:241
  57.4 0.4 shard_map.60
  57.7 32.8 %all_to_all.11 = f32[64,3,2,2,128]{4,3,2,1,0:T(2,128)S(1)} all-to-all(f32[64,3,2,2,128]{4,3,2,1,0:T(2,128)S(1)} %shard_map.60), channel_id=1, replica_groups=mesh['band'=8,'lon'=64] {'lon'}, dimensions={0} | all-to-all | bytes 786432 | tf_op jit(solution)/shard_map/all_to_all | solution.py:183
  90.6 0.9 last.1
Async XLA Ops:
  49.0 8.4 %collective-permute-start = (f32[256,128]{1,0:T(8,128)S(1)}, f32[256,128]{1,0:T(8,128)S(1)}, u32[]{:S(2)}, u32[]{:S(2)}) collective-permute-start(f32[256,128]{1,0:T(8,128)S(1)} %shard_map.56.far_ref.edge_ref), channel_id=1, source_target_pairs={{1,64},{64,1},{3,66},{66,3},{5,68},{68,5},{7,70},{70,7},{9,72},{72... | collective-permute-start | bytes 393224 | tf_op jit(solution)/shard_map/ppermute | solution.py:241
